TPU v7x, 32 devices: a whole 2x2x4 slice. The times are simulated.
32 devices in a mesh: seq: 4 (over y, x), shard: 8 (over z, core).
Axes of the slice: x: 2, y: 2, z: 4, core: 2. Of those that a mesh axis runs over, the one named last changes fastest.
Arguments:
- tokens: bfloat16 [8, 1024, 768], P('shard', 'seq'), may hold values from -6 to 6
- lengths: int32 [8], P('shard'), may hold values from 128 to 1024, as said below
- w_qkv: bfloat16 [768, 2304], P('shard'), may hold values from -0.21875 to 0.21875
- q_bias: bfloat16 [768], P('shard'), may hold values from -3 to 3
- v_bias: bfloat16 [768], P('shard'), may hold values from -3 to 3
- w_out: bfloat16 [768, 768], P('shard'), may hold values from -1.25 to 1.25
- out_bias: bfloat16 [768], P('shard'), may hold values from -3 to 3
- gain_one: bfloat16 [768], P('shard'), may hold values from 0.5 to 1.5
- shift_one: bfloat16 [768], P('shard'), may hold values from -3 to 3
- w_up: bfloat16 [768, 3072], P('shard'), may hold values from -0.21875 to 0.21875
- up_bias: bfloat16 [3072], P('shard'), may hold values from -3 to 3
- w_down: bfloat16 [3072, 768], P('shard'), may hold values from -0.109375 to 0.109375
- down_bias: bfloat16 [768], P('shard'), may hold values from -3 to 3
- gain_two: bfloat16 [768], P('shard'), may hold values from 0.5 to 1.5
- shift_two: bfloat16 [768], P('shard'), may hold values from -3 to 3
- cotangent: bfloat16 [8, 1024, 768], P('shard', 'seq'), may hold values from -6 to 6
Outputs:
- output: bfloat16 [8, 1024, 768], P('shard', 'seq')
- grad_tokens: bfloat16 [8, 1024, 768], P('shard', 'seq')
- grad_w_qkv: float32 [768, 2304], P('shard')
- grad_q_bias: float32 [768], P('shard')
- grad_v_bias: float32 [768], P('shard')
- grad_w_out: float32 [768, 768], P('shard')
- grad_out_bias: float32 [768], P('shard')
- grad_gain_one: float32 [768], P('shard')
- grad_shift_one: float32 [768], P('shard')
- grad_w_up: float32 [768, 3072], P('shard')
- grad_up_bias: float32 [3072], P('shard')
- grad_w_down: float32 [3072, 768], P('shard')
- grad_down_bias: float32 [768], P('shard')
- grad_gain_two: float32 [768], P('shard')
- grad_shift_two: float32 [768], P('shard')
Inputs may be any that keep to these rules, and one draw needn't show every extreme that they name: `lengths`: each sequence has from 128 to 1024 valid positions; in every draw some sequence has exactly 1024 and another exactly 128.
All inputs are finite; a program needn't handle non-finite values.
Results may differ from a plain program's by a relative error of at most 0.015.
Values may be sent and summed in bfloat16 or wider, within the bound.
No kernel may reach another device: no remote copies, remote signals or barrier semaphores. Data moves between devices by JAX's collectives and lax.ppermute only.
A program may use at most 128 MiB of HBM per device.

v0:
```python
import jax
import jax.numpy as jnp
from jax import lax
from jax.sharding import PartitionSpec as P

HEAD_DIM = 64
LEN = 1024
Q_BLOCK = 512


epsilon = 1e-05
masked_score = -1000000000.0


def layer_norm(values, gain, shift):
    center = values - jnp.mean(values, axis=-1, keepdims=True)
    spread = jnp.mean(center * center, axis=-1, keepdims=True)
    return center * lax.rsqrt(spread + epsilon) * gain + shift


def gelu_exact(values):
    return jax.nn.gelu(values, approximate=False)


def contract_rows(left, right):
    return lax.dot_general(
        left, right, (((0,), (0,)), ((), ())), preferred_element_type=jnp.float32
    )


def contract_cols(left, right):
    return lax.dot_general(
        left, right, (((1,), (1,)), ((), ())), preferred_element_type=jnp.float32
    )


def block_scores(q_block, k_seq, key_valid):
    scores = jnp.einsum(
        "qhd,khd->hqk", q_block, k_seq, preferred_element_type=jnp.float32
    ) * HEAD_DIM ** (-0.5)
    return jnp.where(key_valid[None, None, :], scores, masked_score)


def attend_forward(q_seq, k_seq, v_seq, length):
    local_heads = q_seq.shape[1]
    key_valid = jnp.arange(LEN, dtype=jnp.int32) < length
    q_blocks = q_seq.reshape(LEN // Q_BLOCK, Q_BLOCK, local_heads, HEAD_DIM)

    def one_block(q_block):
        scores = block_scores(q_block, k_seq, key_valid)
        row_peak = jnp.max(scores, axis=-1, keepdims=True)
        shifted = jnp.exp(scores - row_peak)
        row_total = jnp.sum(shifted, axis=-1, keepdims=True)
        attn_probs = (shifted / row_total).astype(jnp.bfloat16)
        context = jnp.einsum("hqk,khd->qhd", attn_probs, v_seq, preferred_element_type=jnp.float32)
        return (context.astype(jnp.bfloat16), (row_peak + jnp.log(row_total))[..., 0])

    context, log_total = lax.map(one_block, q_blocks)
    return (context.reshape(LEN, local_heads, HEAD_DIM), log_total)


def attend_backward(q_seq, k_seq, v_seq, grad_seq, log_total, length):
    local_heads = q_seq.shape[1]
    score_scale = HEAD_DIM ** (-0.5)
    key_valid = jnp.arange(LEN, dtype=jnp.int32) < length
    q_blocks = q_seq.reshape(LEN // Q_BLOCK, Q_BLOCK, local_heads, HEAD_DIM)
    g_blocks = grad_seq.reshape(LEN // Q_BLOCK, Q_BLOCK, local_heads, HEAD_DIM)

    def one_block(accum, block_item):
        q_block, g_block, lse_block = block_item
        scores = block_scores(q_block, k_seq, key_valid)
        attn_probs = jnp.exp(scores - lse_block[..., None])
        grad_probs = jnp.einsum("qhd,khd->hqk", g_block, v_seq, preferred_element_type=jnp.float32)
        row_dot = jnp.sum(attn_probs * grad_probs, axis=-1, keepdims=True)
        grad_scores = (attn_probs * (grad_probs - row_dot)).astype(jnp.bfloat16)
        grad_q = (
            jnp.einsum("hqk,khd->qhd", grad_scores, k_seq, preferred_element_type=jnp.float32)
            * score_scale
        )
        grad_k = (
            accum[0]
            + jnp.einsum("hqk,qhd->khd", grad_scores, q_block, preferred_element_type=jnp.float32)
            * score_scale
        )
        grad_v = accum[1] + jnp.einsum(
            "hqk,qhd->khd",
            attn_probs.astype(jnp.bfloat16),
            g_block,
            preferred_element_type=jnp.float32,
        )
        return ((grad_k, grad_v), grad_q.astype(jnp.bfloat16))

    zero_keys = jnp.zeros((LEN, local_heads, HEAD_DIM), jnp.float32)
    (grad_k, grad_v), grad_q = lax.scan(
        one_block, (zero_keys, zero_keys), (q_blocks, g_blocks, log_total)
    )
    return (
        grad_q.reshape(LEN, local_heads, HEAD_DIM),
        grad_k.astype(jnp.bfloat16),
        grad_v.astype(jnp.bfloat16),
    )


def body(
    tokens,
    lengths,
    w_qkv,
    q_bias,
    v_bias,
    w_out,
    out_bias,
    gain_one,
    shift_one,
    w_up,
    up_bias,
    w_down,
    down_bias,
    gain_two,
    shift_two,
    cotangent,
):
    seq_count, local_len, model_width = tokens.shape
    row_count = seq_count * local_len
    head_count = model_width // HEAD_DIM
    gathered = (
        lax.all_gather(w_qkv, "shard", axis=0, tiled=True),
        lax.all_gather(q_bias, "shard", axis=0, tiled=True),
        lax.all_gather(v_bias, "shard", axis=0, tiled=True),
        lax.all_gather(w_out, "shard", axis=0, tiled=True),
        lax.all_gather(out_bias, "shard", axis=0, tiled=True),
        lax.all_gather(gain_one, "shard", axis=0, tiled=True),
        lax.all_gather(shift_one, "shard", axis=0, tiled=True),
        lax.all_gather(w_up, "shard", axis=0, tiled=True),
        lax.all_gather(up_bias, "shard", axis=0, tiled=True),
        lax.all_gather(w_down, "shard", axis=0, tiled=True),
        lax.all_gather(down_bias, "shard", axis=0, tiled=True),
        lax.all_gather(gain_two, "shard", axis=0, tiled=True),
        lax.all_gather(shift_two, "shard", axis=0, tiled=True),
    )
    (
        full_qkv,
        full_q_bias,
        full_v_bias,
        full_out,
        full_out_bias,
        full_gain_one,
        full_shift_one,
        full_up,
        full_up_bias,
        full_down,
        full_down_bias,
        full_gain_two,
        full_shift_two,
    ) = gathered
    token_rows = tokens.reshape(row_count, model_width)
    joined_bias = jnp.concatenate([full_q_bias, jnp.zeros_like(full_q_bias), full_v_bias]).astype(
        jnp.float32
    )
    qkv_rows = (
        jnp.dot(token_rows, full_qkv, preferred_element_type=jnp.float32) + joined_bias
    ).astype(jnp.bfloat16)
    qkv_tokens = qkv_rows.reshape(seq_count, local_len, 3, head_count, HEAD_DIM)
    qkv_heads = lax.all_to_all(qkv_tokens, "seq", split_axis=3, concat_axis=1, tiled=True)

    def forward_seq(seq_item):
        qkv_seq, length = seq_item
        return attend_forward(qkv_seq[:, 0], qkv_seq[:, 1], qkv_seq[:, 2], length)

    context_heads, log_total = lax.map(forward_seq, (qkv_heads, lengths))
    context_tokens = lax.all_to_all(context_heads, "seq", split_axis=1, concat_axis=2, tiled=True)
    context_rows = context_tokens.reshape(row_count, model_width)
    residual_one = (
        token_rows.astype(jnp.float32)
        + jnp.dot(context_rows, full_out, preferred_element_type=jnp.float32)
        + full_out_bias.astype(jnp.float32)
    )
    normed_one, norm_one_pull = jax.vjp(
        layer_norm,
        residual_one,
        full_gain_one.astype(jnp.float32),
        full_shift_one.astype(jnp.float32),
    )
    normed_low = normed_one.astype(jnp.bfloat16)
    up_rows = jnp.dot(
        normed_low, full_up, preferred_element_type=jnp.float32
    ) + full_up_bias.astype(jnp.float32)
    active, gelu_pull = jax.vjp(gelu_exact, up_rows)
    active_low = active.astype(jnp.bfloat16)
    residual_two = (
        normed_one
        + jnp.dot(active_low, full_down, preferred_element_type=jnp.float32)
        + full_down_bias.astype(jnp.float32)
    )
    final_rows, norm_two_pull = jax.vjp(
        layer_norm,
        residual_two,
        full_gain_two.astype(jnp.float32),
        full_shift_two.astype(jnp.float32),
    )
    output = final_rows.astype(jnp.bfloat16).reshape(tokens.shape)
    back_qkv, back_out, back_up, back_down = (full_qkv, full_out, full_up, full_down)
    grad_rows = cotangent.reshape(row_count, model_width).astype(jnp.float32)
    grad_two, grad_gain_two, grad_shift_two = norm_two_pull(grad_rows)
    grad_down_bias = jnp.sum(grad_two, axis=0)
    grad_two_low = grad_two.astype(jnp.bfloat16)
    grad_w_down = contract_rows(active_low, grad_two_low)
    grad_active = contract_cols(grad_two_low, back_down)
    (grad_up,) = gelu_pull(grad_active)
    grad_up_bias = jnp.sum(grad_up, axis=0)
    grad_up_low = grad_up.astype(jnp.bfloat16)
    grad_w_up = contract_rows(normed_low, grad_up_low)
    grad_normed = grad_two + contract_cols(grad_up_low, back_up)
    grad_one, grad_gain_one, grad_shift_one = norm_one_pull(grad_normed)
    grad_out_bias = jnp.sum(grad_one, axis=0)
    grad_one_low = grad_one.astype(jnp.bfloat16)
    grad_w_out = contract_rows(context_rows, grad_one_low)
    grad_context = contract_cols(grad_one_low, back_out).astype(jnp.bfloat16)
    grad_context = grad_context.reshape(seq_count, local_len, head_count, HEAD_DIM)
    grad_context_heads = lax.all_to_all(
        grad_context, "seq", split_axis=2, concat_axis=1, tiled=True
    )

    def backward_seq(seq_item):
        qkv_seq, grad_seq, lse_seq, length = seq_item
        grad_q, grad_k, grad_v = attend_backward(
            qkv_seq[:, 0], qkv_seq[:, 1], qkv_seq[:, 2], grad_seq, lse_seq, length
        )
        return jnp.stack([grad_q, grad_k, grad_v], axis=1)

    grad_qkv_heads = lax.map(backward_seq, (qkv_heads, grad_context_heads, log_total, lengths))
    grad_qkv_tokens = lax.all_to_all(grad_qkv_heads, "seq", split_axis=1, concat_axis=3, tiled=True)
    grad_qkv_rows = grad_qkv_tokens.reshape(row_count, 3 * model_width)
    grad_q_bias = jnp.sum(grad_qkv_rows[:, :model_width], axis=0, dtype=jnp.float32)
    grad_v_bias = jnp.sum(grad_qkv_rows[:, 2 * model_width :], axis=0, dtype=jnp.float32)
    grad_w_qkv = contract_rows(token_rows, grad_qkv_rows)
    grad_tokens = grad_one + contract_cols(grad_qkv_rows, back_qkv)
    grad_tokens = grad_tokens.astype(jnp.bfloat16).reshape(tokens.shape)
    owned = (
        lax.psum_scatter(grad_w_qkv, "shard", scatter_dimension=0, tiled=True),
        lax.psum_scatter(grad_q_bias, "shard", scatter_dimension=0, tiled=True),
        lax.psum_scatter(grad_v_bias, "shard", scatter_dimension=0, tiled=True),
        lax.psum_scatter(grad_w_out, "shard", scatter_dimension=0, tiled=True),
        lax.psum_scatter(grad_out_bias, "shard", scatter_dimension=0, tiled=True),
        lax.psum_scatter(grad_gain_one, "shard", scatter_dimension=0, tiled=True),
        lax.psum_scatter(grad_shift_one, "shard", scatter_dimension=0, tiled=True),
        lax.psum_scatter(grad_w_up, "shard", scatter_dimension=0, tiled=True),
        lax.psum_scatter(grad_up_bias, "shard", scatter_dimension=0, tiled=True),
        lax.psum_scatter(grad_w_down, "shard", scatter_dimension=0, tiled=True),
        lax.psum_scatter(grad_down_bias, "shard", scatter_dimension=0, tiled=True),
        lax.psum_scatter(grad_gain_two, "shard", scatter_dimension=0, tiled=True),
        lax.psum_scatter(grad_shift_two, "shard", scatter_dimension=0, tiled=True),
    )
    owned_columns = (
        lax.psum_scatter(
            owned[0].astype(jnp.bfloat16), "seq", scatter_dimension=1, tiled=True
        ).astype(jnp.float32),
        lax.psum_scatter(
            owned[3].astype(jnp.bfloat16), "seq", scatter_dimension=1, tiled=True
        ).astype(jnp.float32),
        lax.psum_scatter(
            owned[7].astype(jnp.bfloat16), "seq", scatter_dimension=1, tiled=True
        ).astype(jnp.float32),
        lax.psum_scatter(
            owned[9].astype(jnp.bfloat16), "seq", scatter_dimension=1, tiled=True
        ).astype(jnp.float32),
    )
    matrices = (
        lax.all_gather(owned_columns[0].astype(jnp.bfloat16), "seq", axis=1, tiled=True).astype(
            jnp.float32
        ),
        lax.all_gather(owned_columns[1].astype(jnp.bfloat16), "seq", axis=1, tiled=True).astype(
            jnp.float32
        ),
        lax.all_gather(owned_columns[2].astype(jnp.bfloat16), "seq", axis=1, tiled=True).astype(
            jnp.float32
        ),
        lax.all_gather(owned_columns[3].astype(jnp.bfloat16), "seq", axis=1, tiled=True).astype(
            jnp.float32
        ),
    )
    vectors = lax.psum(
        (
            owned[1],
            owned[2],
            owned[4],
            owned[5],
            owned[6],
            owned[8],
            owned[10],
            owned[11],
            owned[12],
        ),
        "seq",
    )
    result_qkv, result_out, result_up, result_down = (
        matrices[0],
        matrices[1],
        matrices[2],
        matrices[3],
    )
    result_q_bias, result_v_bias, result_out_bias = (vectors[0], vectors[1], vectors[2])
    result_gain_one, result_shift_one, result_up_bias = (vectors[3], vectors[4], vectors[5])
    result_down_bias, result_gain_two, result_shift_two = (vectors[6], vectors[7], vectors[8])
    return (
        output,
        grad_tokens,
        result_qkv,
        result_q_bias,
        result_v_bias,
        result_out,
        result_out_bias,
        result_gain_one,
        result_shift_one,
        result_up,
        result_up_bias,
        result_down,
        result_down_bias,
        result_gain_two,
        result_shift_two,
    )


def solution(mesh):
    placed = (
        P("shard", "seq", None),
        P("shard"),
        P("shard", None),
        P("shard"),
        P("shard"),
        P("shard", None),
        P("shard"),
        P("shard"),
        P("shard"),
        P("shard", None),
        P("shard"),
        P("shard", None),
        P("shard"),
        P("shard"),
        P("shard"),
        P("shard", "seq", None),
    )
    return jax.shard_map(
        body,
        mesh=mesh,
        in_specs=placed,
        out_specs=(
            P("shard", "seq", None),
            P("shard", "seq", None),
            P("shard", None),
            P("shard"),
            P("shard"),
            P("shard", None),
            P("shard"),
            P("shard"),
            P("shard"),
            P("shard", None),
            P("shard"),
            P("shard", None),
            P("shard"),
            P("shard"),
            P("shard"),
        ),
        check_vma=False,
    )
```

profile of v0, /device:TPU:0, one launch (start us, length us, event | category | flops | bytes accessed | tf_op | source)
XLA Modules:
  0.0 702.1 jit_solution(10666620002877447919)
XLA Ops:
  18.1 31.6 %all-reduce.19 = (bf16[768]{0:T(1024)(128)(2,1)S(1)}, bf16[768]{0:T(1024)(128)(2,1)S(1)}, bf16[768]{0:T(1024)(128)(2,1)S(1)}, bf16[768]{0:T(1024)(128)(2,1)S(1)}...) all-reduce(bf16[768]{0:T(1024)(128)(2,1)S(1)} %dynamic-update-slice, ...), channel_id=1, replica_groups=mesh['seq'=4,'shard'=8] {'shard'}, use_global_device_ids=true, to_apply=%add.1 | all-reduce | flops 6144 | bytes 24576
  49.7 4.9 all-gather.7.cloned.1.call-done
  54.5 3.2 fusion.47
  59.5 3.6 all-to-all-start
  63.7 15.0 %all-to-all-done = bf16[1,256,3,12,64]{1,4,2,0,3:T(8,128)(2,1)S(1)} async-done(((bf16[1,256,3,12,64]{1,4,2,0,3:T(8,128)(2,1)}), bf16[1,256,3,12,64]{1,4,2,0,3:T(8,128)(2,1)S(1)}, u32[]{:S(2)}, u32[]{:S(2)}) %all-to-all-start) | async-done | bytes 1179680 | tf_op jit(solution)/shard_map/all_to_all | solution.py:163
  82.6 15.9 %while.46 = (s32[]{:T(128)}, bf16[2,512,3,64]{1,3,2,0:T(8,128)(2,1)S(1)}, f32[2,3,512]{2,1,0:T(4,128)}, bf16[2,512,3,64]{1,3,2,0:T(8,128)(2,1)}, bf16[1024,3,64]...) while((s32[]{:T(128)}, bf16[2,512,3,64]{1,3,2,0:T(8,128)(2,1)S(1)}, ...), condition=%wide.region_3.4_spmd.clone, body=%wide.region_0.3_spmd.clone.sunk | while | flops 421625344 | bytes 20113516 | solution.py:58
  83.3 2.0 fusion.128
  85.3 1.6 fusion.129
  86.9 3.0 fusion.130
  91.2 2.0 fusion.128
  93.3 1.6 fusion.129
  94.9 3.0 fusion.130
  99.2 1.4 reshape.255
  100.6 3.5 all-to-all-start.1
  104.1 13.0 %all-gather = bf16[8,1,384]{2,1,0:T(2,128)(2,1)S(1)} all-gather(bf16[1,1,384]{2,1,0:T(2,128)(2,1)S(1)} %reshape.218), channel_id=1, replica_groups=mesh['seq'=4,'shard'=8] {'shard'}, dimensions={0}, use_global_device_ids=true | all-gather | bytes 6912 | tf_op jit(solution)/shard_map/all_gather | solution.py:134
  118.8 1.9 fusion.82
  120.9 10.0 %all-gather.11.cloned.1.call-done = bf16[768,3072]{1,0:T(8,128)(2,1)} async-done(((bf16[96,3072]{1,0:T(8,128)(2,1)}), bf16[768,3072]{1,0:T(8,128)(2,1)}) %all-gather.11.cloned.1.call-update) | async-done | bytes 4718608 | tf_op jit(solution)/shard_map/all_gather | solution.py:133
  130.9 11.6 %multiply_convert_fusion.1 = (bf16[256,3072]{1,0:T(8,128)(2,1)}, f32[256,3072]{1,0:T(8,128)}, f32[256,3072]{1,0:T(8,128)}) fusion(f32[3072]{0:T(1024)S(1)} %bitcast.205, bf16[768,3072]{1,0:T(8,128)(2,1)} %all-gather.11.cloned.1.call-done, f32[256,768]{1,0:T(8,128)S(1)} %get-tuple-element.380, f32[768]{0:T(1024)S(1)} %convert_element_type.136, ...), kind=kOutput, calls=%fused_computation.59 | convolution fusion | flops 1260847104 | bytes 13389824 | tf_op jit(solution)/shard_map/dot_general | solution.py:184
  142.5 40.4 %all-gather.13.cloned.1.call-done = bf16[3072,768]{1,0:T(8,128)(2,1)} async-done(((bf16[384,768]{1,0:T(8,128)(2,1)}), bf16[3072,768]{1,0:T(8,128)(2,1)}) %all-gather.13.cloned.1.call-update) | async-done | bytes 4718608 | tf_op jit(solution)/shard_map/all_gather | solution.py:135
  183.0 4.4 fusion.83
  189.8 2.8 fusion.84
  192.7 2.3 multiply_reduce_fusion.1
  196.8 3.7 all-to-all-start.2
  200.5 1.9 fusion.75
  202.6 5.2 all-to-all-done.2
  209.9 35.1 %while.47 = (s32[]{:T(128)}, f32[1024,3,64]{0,2,1:T(8,128)}, f32[1024,3,64]{0,2,1:T(8,128)}, bf16[2,512,3,64]{1,3,2,0:T(8,128)(2,1)}, bf16[2,512,3,64]{1,3,2,0:T...) while((s32[]{:T(128)}, f32[1024,3,64]{0,2,1:T(8,128)}, ...), condition=%wide.region_14.15_spmd.clone, body=%wide.region_12.14_spmd.clone.sunk | while | flops 1031405056 | bytes 106027344 | solution.py:94
  209.9 1.9 fusion.140
  213.3 3.7 multiply_reduce_fusion.6
  217.0 1.7 multiply_convert_fusion.3
  218.8 2.6 fusion.141
  221.9 3.4 fusion.142
  227.2 1.9 fusion.140
  230.6 3.7 multiply_reduce_fusion.6
  234.3 1.7 multiply_convert_fusion.3
  236.0 2.9 fusion.141
  239.5 3.7 fusion.142
  246.7 1.5 convert_bitcast_fusion.1
  249.3 4.6 copy.90
  253.9 3.1 reshape.257
  257.0 19.6 %all_to_all.60 = bf16[4,2,73728]{2,1,0:T(2,128)(2,1)} all-to-all(bf16[4,2,73728]{2,1,0:T(2,128)(2,1)} %reshape.257), channel_id=1, replica_groups=mesh['seq'=4,'shard'=8] {'seq'}, dimensions={0} | all-to-all | bytes 2359296 | tf_op jit(solution)/shard_map/all_to_all | solution.py:231
  276.6 3.5 reshape.258
  280.1 3.8 copy.101
  283.9 1.5 copy.92
  285.3 4.0 convolution_bitcast_fusion
  289.3 8.0 %copy.102 = f32[768,2304]{1,0:T(8,128)} copy(f32[768,2304]{0,1:T(8,128)} %convolution_bitcast_fusion) | data formatting | bytes 14155776
  299.0 5.2 fusion.64
  305.9 5.2 fusion.73
  313.0 59.1 %reduce-scatter.25.cloned.1.call-done = f32[96,2304]{1,0:T(8,128)} async-done(((f32[768,2304]{1,0:T(8,128)}), f32[96,2304]{1,0:T(8,128)}) %reduce-scatter.25.cloned.1.call-update) | async-done | bytes 884752
  372.1 2.2 copy.103
  374.4 97.8 %reduce-scatter.19.cloned.1.call-done = f32[96,3072]{1,0:T(8,128)} async-done(((f32[768,3072]{1,0:T(8,128)}), f32[96,3072]{1,0:T(8,128)}) %reduce-scatter.19.cloned.1.call-update) | async-done | bytes 1179664 | tf_op jit(solution)/shard_map/reduce_scatter | solution.py:246
  472.3 2.2 convert_element_type.159
  475.8 96.6 %reduce-scatter.23.cloned.1.call-done = f32[384,768]{1,0:T(8,128)} async-done(((f32[3072,768]{1,0:T(8,128)}), f32[384,768]{1,0:T(8,128)}) %reduce-scatter.23.cloned.1.call-update) | async-done | bytes 1179664 | tf_op jit(solution)/shard_map/reduce_scatter | solution.py:248
  572.5 2.2 convert_element_type.161
  574.7 2.1 copy.106
  577.5 26.4 %all-reduce.17 = (f32[768]{0:T(1024)S(1)}, f32[768]{0:T(1024)S(1)}, f32[768]{0:T(1024)S(1)}, f32[768]{0:T(1024)S(1)}, f32[768]{0:T(1024)S(1)}, /*index=5*/f32[30...) all-reduce(f32[768]{0:T(1024)S(1)} %get-tuple-element.301, ...), channel_id=4, replica_groups=mesh['seq'=4,'shard'=8] {'shard'}, use_global_device_ids=true, to_apply=%region_18.19.clone | all-reduce | flops 9216 | bytes 73728
  604.6 10.8 %all-reduce.18 = (f32[96]{0:T(128)}, f32[96]{0:T(128)}, f32[96]{0:T(128)}, f32[96]{0:T(128)}, f32[96]{0:T(128)}, /*index=5*/f32[384]{0:T(512)}, f32[96]{0:T(128)}, f32[96]{0:T(128)}, f32[96]{0:T(128)}) all-reduce(f32[96]{0:T(128)S(1)} %dynamic-slice.10, f32[96]{0:T(128)S(1)} %dynamic-slice.12, ...), channel_id=1, replica_groups=mesh['seq'=4,'shard'=8] {'seq'}, use_global_device_ids=true, to_apply=%region_19.20 | all-reduce | flops 1152 | bytes 9216 | tf_op jit(solution)/shard_map/psum | solution.py:281
  615.4 3.9 fusion.57
  619.4 8.1 %all_gather.65 = bf16[96,768]{0,1:T(8,128)(2,1)S(1)} all-gather(bf16[96,192]{0,1:T(8,128)(2,1)} %bitcast.204), channel_id=1, replica_groups=mesh['seq'=4,'shard'=8] {'seq'}, dimensions={1}, use_global_device_ids=true | all-gather | bytes 184320 | tf_op jit(solution)/shard_map/all_gather | solution.py:271
  629.4 12.0 %all-gather.1 = bf16[4,576,96]{1,2,0:T(8,128)(2,1)S(1)} all-gather(bf16[1,576,96]{1,2,0:T(8,128)(2,1)S(1)} %copy.93), channel_id=1, replica_groups=mesh['seq'=4,'shard'=8] {'seq'}, dimensions={0}, use_global_device_ids=true | all-gather | bytes 552960 | tf_op jit(solution)/shard_map/all_gather | solution.py:268
  641.6 1.5 reshape.239
  643.2 12.3 %reduce-scatter.21.cloned.1.call-done = bf16[96,768]{1,0:T(8,128)(2,1)} async-done(((bf16[96,3072]{1,0:T(8,128)(2,1)}), bf16[96,768]{1,0:T(8,128)(2,1)}) %reduce-scatter.21.cloned.1.call-update) | async-done | bytes 147472 | tf_op jit(solution)/shard_map/reduce_scatter | solution.py:260
  655.5 11.6 %all_gather.66 = bf16[96,3072]{1,0:T(8,128)(2,1)S(1)} all-gather(bf16[96,768]{1,0:T(8,128)(2,1)} %reduce-scatter.21.cloned.1.call-done), channel_id=1, replica_groups=mesh['seq'=4,'shard'=8] {'seq'}, dimensions={1}, use_global_device_ids=true | all-gather | bytes 737280 | tf_op jit(solution)/shard_map/all_gather | solution.py:274
  668.2 15.1 %reduce-scatter.29.cloned.1.call-done = bf16[192,384]{1,0:T(8,128)(2,1)} async-done(((bf16[768,384]{1,0:T(8,128)(2,1)}), bf16[192,384]{1,0:T(8,128)(2,1)}) %reduce-scatter.29.cloned.1.call-update) | async-done | bytes 147472
  683.3 10.2 %all_gather.67 = bf16[384,768]{0,1:T(8,128)(2,1)S(1)} all-gather(bf16[384,192]{0,1:T(8,128)(2,1)} %bitcast.203), channel_id=1, replica_groups=mesh['seq'=4,'shard'=8] {'seq'}, dimensions={1}, use_global_device_ids=true | all-gather | bytes 737280 | tf_op jit(solution)/shard_map/all_gather | solution.py:277
  (216 shorter events, 49.6 us)
Async XLA Ops:
  7.2 47.3 %all-gather.7.cloned.1.call-start = ((), (), s32[]{:S(2)}) async-start(), calls=%async_computation.12 | async-start | bytes 3981312 | tf_op jit(solution)/shard_map/all_gather | solution.py:126
  7.9 110.9 %all-gather.9.cloned.1.call-start = ((), (), s32[]{:S(2)}) async-start(), calls=%async_computation.13 | async-start | bytes 1327104 | tf_op jit(solution)/shard_map/all_gather | solution.py:129
  8.7 122.3 %all-gather.11.cloned.1.call-start = ((), (), s32[]{:S(2)}) async-start(), calls=%async_computation.14 | async-start | bytes 5308416 | tf_op jit(solution)/shard_map/all_gather | solution.py:133
  59.5 19.2 %all-to-all-start = ((bf16[1,256,3,12,64]{1,4,2,0,3:T(8,128)(2,1)}), bf16[1,256,3,12,64]{1,4,2,0,3:T(8,128)(2,1)S(1)}, u32[]{:S(2)}, u32[]{:S(2)}) async-start(bf16[1,256,3,12,64]{1,4,2,0,3:T(8,128)(2,1)} %copy.76), calls=%async_computation | async-start | bytes 2359296 | tf_op jit(solution)/shard_map/all_to_all | solution.py:163
  63.1 119.8 %all-gather.13.cloned.1.call-start = ((), (), s32[]{:S(2)}) async-start(), calls=%async_computation.15 | async-start | bytes 5308416 | tf_op jit(solution)/shard_map/all_gather | solution.py:135
  98.5 5.6 copy-start.32
  99.2 19.6 %copy-start.12 = (bf16[1,256,768]{2,1,0:T(8,128)(2,1)S(1)}, bf16[1,256,768]{2,1,0:T(8,128)(2,1)}, u32[]{:S(2)}) copy-start(bf16[1,256,768]{2,1,0:T(8,128)(2,1)} %param.20) | copy-start | bytes 1179652
  100.6 16.6 %all-to-all-start.1 = ((bf16[4,2,24576]{2,1,0:T(2,128)(2,1)}), bf16[4,2,24576]{2,1,0:T(2,128)(2,1)S(1)}, u32[]{:S(2)}, u32[]{:S(2)}) async-start(bf16[4,2,24576]{2,1,0:T(2,128)(2,1)} %reshape.255), calls=%async_computation.1 | async-start | bytes 786432 | tf_op jit(solution)/shard_map/all_to_all | solution.py:170
  120.7 74.3 %copy-start.4 = (f32[256,768]{1,0:T(8,128)}, f32[256,768]{1,0:T(8,128)S(1)}, u32[]{:S(2)}) copy-start(f32[256,768]{1,0:T(8,128)S(1)} %get-tuple-element.380) | copy-start | bytes 2359300
  120.7 74.3 %copy-start.20 = (f32[256]{0:T(256)}, f32[256]{0:T(256)S(1)}, u32[]{:S(2)}) copy-start(f32[256]{0:T(256)S(1)} %broadcast_multiply_fusion.1) | copy-start | bytes 3076
  120.9 74.1 %copy-start.25 = (f32[256]{0:T(256)}, f32[256]{0:T(256)S(1)}, u32[]{:S(2)}) copy-start(f32[256]{0:T(256)S(1)} %fusion.71) | copy-start | bytes 3076
  182.9 6.8 slice-start.2
  182.9 4.7 copy-start.9
  182.9 6.8 slice-start.3
  182.9 6.9 copy-start.34
  187.4 2.4 copy-start.33
  188.6 4.0 slice-start
  189.8 2.9 copy-start.6
  189.8 2.9 copy-start.28
  189.8 2.8 slice-start.1
  192.6 2.3 copy-start.16
  192.7 2.7 copy-start.8
  195.3 7.2 %copy-start.2 = (f32[256,768]{1,0:T(8,128)}, f32[256,768]{1,0:T(8,128)S(1)}, u32[]{:S(2)}) copy-start(f32[256,768]{1,0:T(8,128)S(1)} %get-tuple-element.364) | copy-start | bytes 2359300
  195.3 7.2 %copy-start.23 = (f32[256]{0:T(256)}, f32[256]{0:T(256)S(1)}, u32[]{:S(2)}) copy-start(f32[256]{0:T(256)S(1)} %negate_multiply_fusion.1) | copy-start | bytes 3076
  196.8 10.9 %all-to-all-start.2 = ((bf16[1,256,12,64]{1,3,0,2:T(8,128)(2,1)}), bf16[1,256,12,64]{1,3,0,2:T(8,128)(2,1)S(1)}, u32[]{:S(2)}, u32[]{:S(2)}) async-start(bf16[1,256,12,64]{1,3,0,2:T(8,128)(2,1)} %bitcast.16), calls=%async_computation.2 | async-start | bytes 786432 | tf_op jit(solution)/shard_map/all_to_all | solution.py:219
  200.5 110.6 %reduce-scatter.17.cloned.1.call-start = ((), (), s32[]{:S(2)}) async-start(), calls=%async_computation.17 | async-start | bytes 2654208 | tf_op jit(solution)/shard_map/reduce_scatter | solution.py:242
  202.5 169.6 %reduce-scatter.25.cloned.1.call-start = ((), (), s32[]{:S(2)}) async-start(), calls=%async_computation.21 | async-start | bytes 7962624
  211.9 5.1 copy-start
  213.3 3.7 copy-start.18
  218.7 3.2 copy-start.1
  218.8 3.2 copy-start.19
  221.9 3.4 copy-start.14
  226.4 0.8 copy-start.15
  229.1 5.2 copy-start
  230.6 3.7 copy-start.18
  236.0 3.5 copy-start.1
  236.0 3.5 copy-start.19
  239.5 3.7 copy-start.14
  244.2 0.8 copy-start.15
  280.1 5.3 copy-start.13
  297.4 1.1 copy-start.5
  297.4 1.7 copy-start.17
  297.4 1.7 copy-start.21
  297.4 1.7 copy-start.26
  297.4 174.9 %reduce-scatter.19.cloned.1.call-start = ((), (), s32[]{:S(2)}) async-start(), calls=%async_computation.18 | async-start | bytes 10616832 | tf_op jit(solution)/shard_map/reduce_scatter | solution.py:246
  304.2 1.1 copy-start.7
  304.2 1.7 copy-start.11
  304.2 1.7 copy-start.29
  304.3 268.2 %reduce-scatter.23.cloned.1.call-start = ((), (), s32[]{:S(2)}) async-start(), calls=%async_computation.20 | async-start | bytes 10616832 | tf_op jit(solution)/shard_map/reduce_scatter | solution.py:248
  311.1 308.3 %reduce-scatter.27.cloned.1.call-start = ((), (), s32[]{:S(2)}) async-start(), calls=%async_computation.22 | async-start | bytes 245760
  313.0 315.4 %reduce-scatter.15.cloned.1.call-start = ((), (), s32[]{:S(2)}) async-start(), calls=%async_computation.16 | async-start | bytes 737280 | tf_op jit(solution)/shard_map/reduce_scatter | solution.py:254
  374.3 202.5 %copy-start.10 = (bf16[1,256,768]{2,1,0:T(8,128)(2,1)S(1)}, bf16[1,256,768]{2,1,0:T(8,128)(2,1)}, u32[]{:S(2)}) copy-start(bf16[1,256,768]{2,1,0:T(8,128)(2,1)} %param.35) | copy-start | bytes 1179652
  374.4 202.6 %copy-start.3 = (f32[256,768]{1,0:T(8,128)S(1)}, f32[256,768]{1,0:T(8,128)}, u32[]{:S(2)}) copy-start(f32[256,768]{1,0:T(8,128)} %copy-done.2) | copy-start | bytes 2359300
  374.4 202.6 %copy-start.24 = (f32[256]{0:T(256)S(1)}, f32[256]{0:T(256)}, u32[]{:S(2)}) copy-start(f32[256]{0:T(256)} %copy-done.23) | copy-start | bytes 3076
  374.4 281.1 %reduce-scatter.21.cloned.1.call-start = ((), (), s32[]{:S(2)}) async-start(), calls=%async_computation.19 | async-start | bytes 737280 | tf_op jit(solution)/shard_map/reduce_scatter | solution.py:260
  474.5 208.9 %reduce-scatter.29.cloned.1.call-start = ((), (), s32[]{:S(2)}) async-start(), calls=%async_computation.23 | async-start | bytes 737280
  475.8 101.7 %copy-start.22 = (f32[768]{0:T(1024)S(1)}, f32[768]{0:T(1024)}, u32[]{:S(2)}) copy-start(f32[768]{0:T(1024)} %get-tuple-element.298) | copy-start | bytes 9220
  475.8 101.7 %copy-start.27 = (f32[3072]{0:T(1024)S(1)}, f32[3072]{0:T(1024)}, u32[]{:S(2)}) copy-start(f32[3072]{0:T(1024)} %get-tuple-element.385) | copy-start | bytes 36868
  475.8 101.7 %copy-start.30 = (f32[768]{0:T(1024)S(1)}, f32[768]{0:T(1024)}, u32[]{:S(2)}) copy-start(f32[768]{0:T(1024)} %get-tuple-element.296) | copy-start | bytes 9220
  475.8 101.7 %copy-start.31 = (f32[768]{0:T(1024)S(1)}, f32[768]{0:T(1024)}, u32[]{:S(2)}) copy-start(f32[768]{0:T(1024)} %get-tuple-element.302) | copy-start | bytes 9220
Sparse Core Ops, SparseCore 0:
  9.7 44.8 all-gather.6
  56.2 21.5 all-gather.8
  79.4 51.5 all-gather.10
  132.4 50.4 all-gather.12
  203.3 35.7 reduce-scatter.16
  297.5 74.5 reduce-scatter.24
  374.4 97.8 reduce-scatter.18
  474.6 97.8 reduce-scatter.22
  575.8 22.3 reduce-scatter.26
  601.5 25.3 reduce-scatter.14
  630.6 24.8 reduce-scatter.20
  658.2 25.0 reduce-scatter.28
where the time goes:
time: 711 us; the launch traced here: 702 us
  waiting for transfers between devices  359 us (50%)
  blocking collectives  143 us (20%)
  matrix products  83 us (12%)
  local copies, waits for them, and re-layouts  64.3 us (9%)
  other arithmetic  23.2 us (3%)
  between operations  17.3 us (2%)
  starting transfers between devices  11.5 us (2%)
    reduce_scatter x1, waiting for transfers between devices, body(): lax.psum_scatter(grad_w_up, 'shard', scatter_dimension=0, tiled=True)  97.8 us
    reduce_scatter x1, waiting for transfers between devices, body(): lax.psum_scatter(grad_w_down, 'shard', scatter_dimension=0, tiled=True)  96.6 us
    unnamed x15, waiting for transfers between devices  76.9 us
    unnamed x2, blocking collectives  58 us
    all_gather x1, waiting for transfers between devices, body(): lax.all_gather(w_down, 'shard', axis=0, tiled=True)  40.4 us
    unnamed x107, local copies, waits for them, and re-layouts  38.5 us
    all_to_all x1, blocking collectives, body(): lax.all_to_all(grad_qkv_heads, 'seq', split_axis=1, concat_axis=3, tiled=...  19.6 us
    dot_general x4, matrix products, contract_rows(): lax.dot_general(left, right, (((0,), (0,)), ((), ())), preferred_element_...  16.3 us
  transfers between devices with their start and end apart: 15, of which 10 were waited for; matrix products, arithmetic and copies ran while one was open for 21% of the time, Pallas kernels for 0%

commit v1 on v0

--- a/solution.py
+++ b/solution.py
@@ -1,6 +1,8 @@
 import jax
 import jax.numpy as jnp
 from jax import lax
+from jax.experimental import pallas as pl
+from jax.experimental.pallas import tpu as pltpu
 from jax.sharding import PartitionSpec as P
 
 HEAD_DIM = 64
@@ -320,45 +322,642 @@
     )
 
 
+AXES = ("seq", "z", "core")
+NORMAL_SCALE = 0.3989422804014327
+HALF_ROOT = 0.7071067811865476
+
+
+def dot_nn(left, right):
+    return lax.dot_general(
+        left, right, (((1,), (0,)), ((), ())), preferred_element_type=jnp.float32
+    )
+
+
+def dot_nt(left, right):
+    return contract_cols(left, right)
+
+
+def dot_tn(left, right):
+    return contract_rows(left, right)
+
+
+def vmem_specs(count):
+    return [pl.BlockSpec(memory_space=pltpu.VMEM)] * count
+
+
+def smem_spec():
+    return pl.BlockSpec(memory_space=pltpu.SMEM)
+
+
+def key_bias(sc, block_rows):
+    length, place = sc[0], sc[1]
+    columns = []
+    for j in range(4):
+        position = (place ^ j) * block_rows + lax.broadcasted_iota(
+            jnp.int32, (block_rows, 1), 0
+        )
+        columns.append(jnp.where(position < length, 0.0, masked_score))
+    return jnp.concatenate(columns, axis=0)
+
+
+def attend_forward_kernel(
+    sc, t0, t1, t2, t3, own, other, qkv, ctx_t, c0, c1, c2, c3, lse, weight
+):
+    place, core = sc[1], sc[2]
+    rows = t0.shape[0]
+    shard_rows = weight.shape[2]
+    width = weight.shape[3]
+    head_width = width // 3
+    heads = head_width // HEAD_DIM
+    weight[:, pl.ds(core, 1)] = own[:, :shard_rows, :][:, None]
+    weight[:, pl.ds(1 - core, 1)] = other[:, :shard_rows, :][:, None]
+    full = weight[...].reshape(-1, width)
+    bias = (
+        own[place, shard_rows : shard_rows + 1, :].astype(jnp.float32)
+        + other[place, shard_rows : shard_rows + 1, :].astype(jnp.float32)
+    )
+    for j, block in enumerate((t0, t1, t2, t3)):
+        qkv[j * rows : (j + 1) * rows, :] = (dot_nn(block[...], full) + bias).astype(jnp.bfloat16)
+    mask = key_bias(sc, rows)
+    for j, out in enumerate((c0, c1, c2, c3)):
+        parts = []
+        q_all = qkv[j * rows : (j + 1) * rows, 0:head_width] * jnp.bfloat16(HEAD_DIM**-0.5)
+        for h in range(heads):
+            low = h * HEAD_DIM
+            q = q_all[:, low : low + HEAD_DIM]
+            k = qkv[:, head_width + low : head_width + low + HEAD_DIM]
+            v = qkv[:, 2 * head_width + low : 2 * head_width + low + HEAD_DIM]
+            scores = dot_nt(k, q) + mask
+            peak = jnp.max(scores, axis=0, keepdims=True)
+            shifted = jnp.exp(scores - peak)
+            total = jnp.sum(shifted, axis=0, keepdims=True)
+            part = dot_tn(v, shifted.astype(jnp.bfloat16)) / total
+            parts.append(part)
+            lse[h : h + 1, j * rows : (j + 1) * rows] = peak + jnp.log(total)
+        joined = jnp.concatenate(parts, axis=0)
+        ctx_t[:, j * rows : (j + 1) * rows] = joined
+        out[...] = joined.T.astype(jnp.bfloat16)
+
+
+def attend_backward_kernel(sc, qkv, ctx_t, lse, g0, g1, g2, g3, dqkv, dk_acc, dv_acc):
+    rows = g0.shape[0]
+    head_width = g0.shape[1]
+    heads = head_width // HEAD_DIM
+    mask = key_bias(sc, rows)
+    scale = jnp.bfloat16(HEAD_DIM**-0.5)
+    for j, g_ref in enumerate((g0, g1, g2, g3)):
+        span = slice(j * rows, (j + 1) * rows)
+        g_all = g_ref[...]
+        product = g_all.astype(jnp.float32).T * ctx_t[:, span]
+        q_all = qkv[span, 0:head_width] * scale
+        parts = []
+        for h in range(heads):
+            low = h * HEAD_DIM
+            q = q_all[:, low : low + HEAD_DIM]
+            g = g_all[:, low : low + HEAD_DIM]
+            k = qkv[:, head_width + low : head_width + low + HEAD_DIM]
+            v = qkv[:, 2 * head_width + low : 2 * head_width + low + HEAD_DIM]
+            probs = jnp.exp(dot_nt(k, q) + mask - lse[h : h + 1, span])
+            row_dot = jnp.sum(product[low : low + HEAD_DIM, :], axis=0, keepdims=True)
+            grad_scores = (probs * (dot_nt(v, g) - row_dot)).astype(jnp.bfloat16)
+            grad_v = dot_nn(probs.astype(jnp.bfloat16), g)
+            grad_k = dot_nn(grad_scores, q)
+            if j == 0:
+                dv_acc[h] = grad_v
+                dk_acc[h] = grad_k
+            else:
+                dv_acc[h] += grad_v
+                dk_acc[h] += grad_k
+            parts.append(dot_tn(k, grad_scores) * (HEAD_DIM**-0.5))
+        dqkv[span, 0:head_width] = jnp.concatenate(parts, axis=0).T.astype(jnp.bfloat16)
+    dk = jnp.concatenate([dk_acc[h] for h in range(heads)], axis=1)
+    dv = jnp.concatenate([dv_acc[h] for h in range(heads)], axis=1)
+    dqkv[:, head_width:] = jnp.concatenate([dk, dv], axis=1).astype(jnp.bfloat16)
+
+
+def grad_qkv_weight_kernel(sc, t0, t1, t2, t3, dqkv, keep, send, sums):
+    core = sc[2]
+    rows = t0.shape[0]
+    total = None
+    for j, block in enumerate((t0, t1, t2, t3)):
+        part = dot_tn(block[...], dqkv[j * rows : (j + 1) * rows, :])
+        total = part if total is None else total + part
+    sums[...] = jnp.sum(dqkv[...].astype(jnp.float32), axis=0, keepdims=True)
+    shard_rows = keep.shape[1]
+    low = total.astype(jnp.bfloat16)
+    for z in range(keep.shape[0]):
+        even = low[(2 * z) * shard_rows : (2 * z + 1) * shard_rows]
+        odd = low[(2 * z + 1) * shard_rows : (2 * z + 2) * shard_rows]
+        keep[z] = jnp.where(core == 0, even, odd)
+        send[z] = jnp.where(core == 0, odd, even)
+
+
+def grad_tokens_kernel(dqkv, weight, o0, o1, o2, o3):
+    rows = o0.shape[0]
+    full = weight[...].reshape(-1, weight.shape[3])
+    for j, out in enumerate((o0, o1, o2, o3)):
+        part = dot_nt(dqkv[j * rows : (j + 1) * rows, :], full)
+        out[...] = part.astype(out.dtype)
+
+
+def normalize(values):
+    center = values - jnp.mean(values, axis=-1, keepdims=True)
+    inverse = lax.rsqrt(jnp.mean(center * center, axis=-1, keepdims=True) + epsilon)
+    return center * inverse, inverse
+
+
+def normalize_back(grad, unit, inverse):
+    return inverse * (
+        grad
+        - jnp.mean(grad, axis=-1, keepdims=True)
+        - unit * jnp.mean(grad * unit, axis=-1, keepdims=True)
+    )
+
+
+def middle_kernel(
+    sc,
+    x0,
+    x1,
+    x2,
+    x3,
+    token,
+    cotangent,
+    own_out,
+    other_out,
+    small,
+    up_bias,
+    gathered,
+    output,
+    grad_one,
+    y0,
+    y1,
+    y2,
+    y3,
+    keep,
+    send,
+    sums,
+    up_sums,
+    w_out,
+    w_up,
+    w_down,
+    slope,
+    active,
+    grad_up,
+    context,
+    sems,
+):
+    place, core = sc[1], sc[2]
+    blocks = w_up.shape[0]
+    shard_rows = w_up.shape[2]
+    width = w_up.shape[3]
+    copies = []
+    for b in range(blocks):
+        copies.append(
+            pltpu.make_async_copy(gathered.at[:, b, 0:shard_rows, :], w_up.at[b], sems.at[b])
+        )
+    copies.append(
+        pltpu.make_async_copy(
+            gathered.at[:, :, shard_rows : 2 * shard_rows, :], w_down, sems.at[blocks]
+        )
+    )
+    for copy in copies:
+        copy.start()
+    w_out[:, pl.ds(core, 1)] = own_out[:, :shard_rows, :][:, None]
+    w_out[:, pl.ds(1 - core, 1)] = other_out[:, :shard_rows, :][:, None]
+    out_rows = 2 * shard_rows
+
+    def out_block(j):
+        return w_out[place ^ j].reshape(out_rows, width)
+
+    residual = token[...].astype(jnp.float32) + small[0:1, :]
+    for j, block in enumerate((x0, x1, x2, x3)):
+        residual = residual + dot_nn(block[...], out_block(j))
+    unit_one, inverse_one = normalize(residual)
+    gain_one = small[1:2, :]
+    normed = unit_one * gain_one + small[2:3, :]
+    normed_low = normed.astype(jnp.bfloat16)
+    for b in range(blocks):
+        copies[b].wait()
+        span = slice(b * width, (b + 1) * width)
+        up = dot_nn(normed_low, w_up[b].reshape(width, width)) + up_bias[:, span]
+        phi = 0.5 + 0.5 * lax.erf(up * HALF_ROOT)
+        slope[:, span] = phi + up * (jnp.exp(-0.5 * up * up) * NORMAL_SCALE)
+        active[:, span] = (up * phi).astype(jnp.bfloat16)
+    copies[blocks].wait()
+    residual = normed + small[3:4, :] + dot_nn(active[...], w_down[...].reshape(-1, width))
+    unit_two, inverse_two = normalize(residual)
+    gain_two = small[4:5, :]
+    output[...] = (unit_two * gain_two + small[5:6, :]).astype(jnp.bfloat16)
+    grad = cotangent[...].astype(jnp.float32)
+    sums[3:4, :] = jnp.sum(grad * unit_two, axis=0, keepdims=True)
+    sums[4:5, :] = jnp.sum(grad, axis=0, keepdims=True)
+    grad_two = normalize_back(grad * gain_two, unit_two, inverse_two)
+    sums[5:6, :] = jnp.sum(grad_two, axis=0, keepdims=True)
+    two_low = grad_two.astype(jnp.bfloat16)
+    grad_normed = grad_two
+    per_block = w_down.shape[0] // blocks
+    for b in range(blocks):
+        span = slice(b * width, (b + 1) * width)
+        rows_down = w_down[b * per_block : (b + 1) * per_block].reshape(width, width)
+        part = dot_nt(two_low, rows_down) * slope[:, span]
+        up_sums[:, span] = jnp.sum(part, axis=0, keepdims=True)
+        part = part.astype(jnp.bfloat16)
+        grad_up[:, span] = part
+        grad_normed = grad_normed + dot_nt(part, w_up[b].reshape(width, width))
+    sums[1:2, :] = jnp.sum(grad_normed * unit_one, axis=0, keepdims=True)
+    sums[2:3, :] = jnp.sum(grad_normed, axis=0, keepdims=True)
+    first = normalize_back(grad_normed * gain_one, unit_one, inverse_one)
+    sums[0:1, :] = jnp.sum(first, axis=0, keepdims=True)
+    sums[6:8, :] = jnp.zeros((2, width), jnp.float32)
+    grad_one[...] = first
+    one_low = first.astype(jnp.bfloat16)
+    for j, out in enumerate((y0, y1, y2, y3)):
+        out[...] = dot_nt(one_low, out_block(j)).astype(jnp.bfloat16)
+    for j, block in enumerate((x0, x1, x2, x3)):
+        context[place ^ j] = block[...]
+    joined = jnp.concatenate([context[j] for j in range(4)], axis=1)
+    half = width // 2
+    down_rows = blocks * shard_rows
+    for ref, mine in ((keep, core), (send, 1 - core)):
+        for z in range(4):
+            even = active[:, (2 * z) * down_rows : (2 * z + 1) * down_rows]
+            odd = active[:, (2 * z + 1) * down_rows : (2 * z + 2) * down_rows]
+            ref[:, z * down_rows : (z + 1) * down_rows] = jnp.where(mine == 0, even, odd)
+        at = 4 * down_rows
+        ref[:, at : at + width] = two_low
+        at += width
+        ref[:, at : at + width] = normed_low
+        at += width
+        ref[:, at : at + 2 * width] = jnp.where(
+            mine == 0, grad_up[:, : 2 * width], grad_up[:, 2 * width :]
+        )
+        at += 2 * width
+        ref[:, at : at + width] = joined
+        at += width
+        ref[:, at : at + half] = jnp.where(mine == 0, one_low[:, :half], one_low[:, half:])
+
+
+def weight_grads_kernel(keep, got, g_down, g_up, g_out):
+    width = g_down.shape[3]
+    shard_rows = g_down.shape[2]
+    zs = g_down.shape[1]
+    ss = g_down.shape[0]
+    half = width // 2
+    down_rows = ss * shard_rows
+    at_two = zs * down_rows
+    at_norm = at_two + width
+    at_up = at_norm + width
+    at_ctx = at_up + 2 * width
+    at_one = at_ctx + width
+
+    def pair(left, right):
+        return dot_tn(keep[:, left], keep[:, right]) + dot_tn(got[:, left], got[:, right])
+
+    for z in range(zs):
+        part = pair(
+            slice(z * down_rows, (z + 1) * down_rows), slice(at_two, at_two + width)
+        ).astype(jnp.bfloat16)
+        for s in range(ss):
+            g_down[s, z] = part[s * shard_rows : (s + 1) * shard_rows]
+    up_cols = g_up.shape[3]
+    for s in range(ss):
+        part = pair(
+            slice(at_norm, at_norm + width),
+            slice(at_up + s * up_cols, at_up + (s + 1) * up_cols),
+        ).astype(jnp.bfloat16)
+        for z in range(zs):
+            g_up[s, z] = part[2 * z * shard_rows : (2 * z + 2) * shard_rows]
+    part = pair(slice(at_ctx, at_ctx + width), slice(at_one, at_one + half)).astype(jnp.bfloat16)
+    for z in range(zs):
+        g_out[z] = part[2 * z * shard_rows : (2 * z + 2) * shard_rows]
+
+
+def fast_body(
+    tokens,
+    lengths,
+    w_qkv,
+    q_bias,
+    v_bias,
+    w_out,
+    out_bias,
+    gain_one,
+    shift_one,
+    w_up,
+    up_bias,
+    w_down,
+    down_bias,
+    gain_two,
+    shift_two,
+    cotangent,
+):
+    bf16, f32 = jnp.bfloat16, jnp.float32
+    _, rows, width = tokens.shape
+    shard_rows = w_qkv.shape[0]
+    hidden = w_up.shape[1]
+    head_width = width // 4
+    place = lax.axis_index("seq")
+    core = lax.axis_index("core")
+    zs = 4
+    swap = [(0, 1), (1, 0)]
+
+    def struct(shape, dtype=bf16):
+        return jax.ShapeDtypeStruct(shape, dtype)
+
+    def across(value, step):
+        return lax.ppermute(value, "seq", [(i, i ^ step) for i in range(4)])
+
+    def partner(value):
+        return lax.ppermute(value, "core", swap)
+
+    def spread(value, axis):
+        copies = jnp.broadcast_to(value[None], (4,) + value.shape)
+        return lax.all_to_all(copies, axis, split_axis=0, concat_axis=0, tiled=True)
+
+    token = tokens[0]
+    quarter = jnp.concatenate(
+        [
+            lax.dynamic_slice_in_dim(w_up, place * width, width, axis=1),
+            lax.dynamic_slice_in_dim(w_down, place * shard_rows, shard_rows, axis=0),
+        ],
+        axis=0,
+    )
+    gathered = lax.all_gather(quarter, ("z", "core", "seq"), axis=0, tiled=True)
+    gathered = gathered.reshape(2 * zs, 4, 2 * shard_rows, width)
+    columns = lax.dynamic_index_in_dim(
+        w_qkv.reshape(shard_rows, 3, 4, head_width), place, axis=2, keepdims=False
+    ).reshape(shard_rows, 3 * head_width)
+    pair_rows = jnp.zeros((2, 2, shard_rows), bf16)
+    placed_q = lax.dynamic_update_slice(pair_rows[0], q_bias[None], (core, 0)).reshape(1, -1)
+    placed_v = lax.dynamic_update_slice(pair_rows[0], v_bias[None], (core, 0)).reshape(1, -1)
+    bias_row = jnp.concatenate(
+        [placed_q, jnp.zeros((1, head_width), bf16), placed_v], axis=1
+    )
+    own_block = jnp.concatenate(
+        [columns, bias_row, jnp.zeros((15, 3 * head_width), bf16)], axis=0
+    )
+    t1, t2, t3 = across(token, 1), across(token, 2), across(token, 3)
+    own_cols = spread(own_block, "z")
+    other_cols = partner(own_cols)
+    sc = jnp.stack([lengths[0], place, core]).astype(jnp.int32)
+    all_rows = 4 * rows
+    qkv, ctx_t, c0, c1, c2, c3, lse, full_qkv = pl.pallas_call(
+        attend_forward_kernel,
+        name="attend_forward",
+        out_shape=(
+            struct((all_rows, 3 * head_width)),
+            struct((head_width, all_rows), f32),
+            struct((rows, head_width)),
+            struct((rows, head_width)),
+            struct((rows, head_width)),
+            struct((rows, head_width)),
+            struct((head_width // HEAD_DIM, all_rows), f32),
+            struct((zs, 2, shard_rows, 3 * head_width)),
+        ),
+        in_specs=[smem_spec()] + vmem_specs(6),
+        out_specs=tuple(vmem_specs(8)),
+    )(sc, token, t1, t2, t3, own_cols, other_cols)
+    vectors = jnp.concatenate(
+        [out_bias, gain_one, shift_one, down_bias, gain_two, shift_two, up_bias]
+    )
+    pad = 16 * width - vectors.shape[0]
+    out_shard = jnp.concatenate(
+        [w_out, jnp.pad(vectors, (0, pad)).reshape(16, width)], axis=0
+    )
+    own_out = spread(out_shard, "z")
+    other_out = partner(own_out)
+    x1, x2, x3 = across(c1, 1), across(c2, 2), across(c3, 3)
+    own_vec = own_out[:, shard_rows : shard_rows + 2].reshape(zs, -1)[:, : vectors.shape[0]]
+    other_vec = other_out[:, shard_rows : shard_rows + 2].reshape(zs, -1)[:, : vectors.shape[0]]
+    first = core == 0
+    all_vec = jnp.stack(
+        [jnp.where(first, own_vec, other_vec), jnp.where(first, other_vec, own_vec)], axis=1
+    ).astype(f32)
+    all_vec = all_vec.reshape(2 * zs, -1)
+    six = all_vec[:, : 6 * shard_rows].reshape(2 * zs, 6, shard_rows)
+    six = six.transpose(1, 0, 2).reshape(6, width)
+    small = jnp.concatenate([six, jnp.zeros((2, width), f32)], axis=0)
+    full_up_bias = all_vec[:, 6 * shard_rows :].reshape(1, hidden)
+    packed = hidden // 2 + 5 * width + width // 2
+    output, grad_one, y0, y1, y2, y3, keep, send, sums, up_sums = pl.pallas_call(
+        middle_kernel,
+        name="middle",
+        out_shape=(
+            struct((rows, width)),
+            struct((rows, width), f32),
+            struct((rows, head_width)),
+            struct((rows, head_width)),
+            struct((rows, head_width)),
+            struct((rows, head_width)),
+            struct((rows, packed)),
+            struct((rows, packed)),
+            struct((8, width), f32),
+            struct((1, hidden), f32),
+        ),
+        in_specs=[smem_spec()]
+        + vmem_specs(10)
+        + [pl.BlockSpec(memory_space=pl.ANY)],
+        out_specs=tuple(vmem_specs(10)),
+        scratch_shapes=[
+            pltpu.VMEM((zs, 2, shard_rows, width), bf16),
+            pltpu.VMEM((4, 2 * zs, shard_rows, width), bf16),
+            pltpu.VMEM((2 * zs, 4, shard_rows, width), bf16),
+            pltpu.VMEM((rows, hidden), f32),
+            pltpu.VMEM((rows, hidden), bf16),
+            pltpu.VMEM((rows, hidden), bf16),
+            pltpu.VMEM((4, rows, head_width), bf16),
+            pltpu.SemaphoreType.DMA((5,)),
+        ],
+    )(
+        sc,
+        c0,
+        x1,
+        x2,
+        x3,
+        token,
+        cotangent[0],
+        own_out,
+        other_out,
+        small,
+        full_up_bias,
+        gathered,
+    )
+    g1, g2, g3 = across(y1, 1), across(y2, 2), across(y3, 3)
+    got = partner(send)
+    g_down, g_up, g_out = pl.pallas_call(
+        weight_grads_kernel,
+        name="weight_grads",
+        out_shape=(
+            struct((4, zs, shard_rows, width)),
+            struct((4, zs, 2 * shard_rows, hidden // 8)),
+            struct((zs, 2 * shard_rows, width // 2)),
+        ),
+        in_specs=vmem_specs(2),
+        out_specs=tuple(vmem_specs(3)),
+    )(keep, got)
+
+    def exchange(value, axis):
+        return lax.all_to_all(value, axis, split_axis=0, concat_axis=0, tiled=True)
+
+    def total(value):
+        return jnp.sum(value.astype(f32), axis=0).astype(bf16)
+
+    down_part = total(exchange(g_down, "seq"))
+    up_part = total(exchange(g_up, "seq"))
+    down_part = total(exchange(down_part, "z"))
+    up_part = total(exchange(up_part, "z"))
+    out_part = total(exchange(g_out, "z"))
+
+    dqkv = pl.pallas_call(
+        attend_backward_kernel,
+        name="attend_backward",
+        out_shape=struct((all_rows, 3 * head_width)),
+        in_specs=[smem_spec()] + vmem_specs(7),
+        out_specs=pl.BlockSpec(memory_space=pltpu.VMEM),
+        scratch_shapes=[
+            pltpu.VMEM((head_width // HEAD_DIM, all_rows, HEAD_DIM), f32),
+            pltpu.VMEM((head_width // HEAD_DIM, all_rows, HEAD_DIM), f32),
+        ],
+    )(sc, qkv, ctx_t, lse, y0, g1, g2, g3)
+    q_keep, q_send, q_sums = pl.pallas_call(
+        grad_qkv_weight_kernel,
+        name="grad_qkv_weight",
+        out_shape=(
+            struct((zs, shard_rows, 3 * head_width)),
+            struct((zs, shard_rows, 3 * head_width)),
+            struct((1, 3 * head_width), f32),
+        ),
+        in_specs=[smem_spec()] + vmem_specs(5),
+        out_specs=tuple(vmem_specs(3)),
+    )(sc, token, t1, t2, t3, dqkv)
+    q_got = partner(q_send)
+    o0, o1, o2, o3 = pl.pallas_call(
+        grad_tokens_kernel,
+        name="grad_tokens",
+        out_shape=(
+            struct((rows, width), f32),
+            struct((rows, width)),
+            struct((rows, width)),
+            struct((rows, width)),
+        ),
+        in_specs=vmem_specs(2),
+        out_specs=tuple(vmem_specs(4)),
+    )(dqkv, full_qkv)
+    q_part = (q_keep.astype(f32) + q_got.astype(f32)).astype(bf16)
+    q_part = total(exchange(q_part, "z"))
+    r1, r2, r3 = across(o1, 1), across(o2, 2), across(o3, 3)
+    grad_tokens = (
+        (grad_one + o0) + r1.astype(f32) + r2.astype(f32) + r3.astype(f32)
+    ).astype(bf16)
+
+    q_row = lax.dynamic_update_slice(
+        jnp.zeros((1, width), f32), q_sums[:, :head_width], (0, place * head_width)
+    )
+    v_row = lax.dynamic_update_slice(
+        jnp.zeros((1, width), f32), q_sums[:, 2 * head_width :], (0, place * head_width)
+    )
+
+    def everywhere(value):
+        value = value + partner(value)
+        value = value + across(value, 1)
+        value = value + across(value, 2)
+        for step in (1, 2):
+            value = value + lax.ppermute(value, "z", [(i, i ^ step) for i in range(4)])
+        return value
+
+    early = everywhere(jnp.concatenate([sums[:6], up_sums.reshape(4, width)], axis=0))
+    late = everywhere(jnp.concatenate([q_row, v_row], axis=0))
+    shard = 2 * lax.axis_index("z") + core
+
+    def owned(vector):
+        size = vector.shape[0] // (2 * zs)
+        return lax.dynamic_slice(vector, (shard * size,), (size,))
+
+    up_two = up_part.reshape(2, shard_rows, hidden // 8)
+    out_two = out_part.reshape(2, shard_rows, width // 2)
+    out_two = total(spread(out_two, "seq"))
+
+    def both_halves(value):
+        mine = lax.dynamic_index_in_dim(value, core, axis=0, keepdims=False)
+        theirs = lax.dynamic_index_in_dim(value, 1 - core, axis=0, keepdims=False)
+        theirs = partner(theirs)
+        return jnp.where(first, mine, theirs), jnp.where(first, theirs, mine)
+
+    up_left, up_right = both_halves(up_two)
+    out_left, out_right = both_halves(out_two)
+    result_out = jnp.concatenate([out_left, out_right], axis=1).astype(f32)
+    joined = jnp.concatenate(
+        [down_part, jnp.concatenate([up_left, up_right], axis=1)], axis=0
+    )
+    blocks = spread(joined, "seq").astype(f32)
+    result_down = blocks[:, :shard_rows].reshape(4 * shard_rows, width)
+    up_blocks = blocks[:, shard_rows:].reshape(4, shard_rows, 2, hidden // 8)
+    result_up = up_blocks.transpose(1, 2, 0, 3).reshape(shard_rows, hidden)
+    q_blocks = spread(q_part, "seq").astype(f32).reshape(4, shard_rows, 3, head_width)
+    result_qkv = q_blocks.transpose(1, 2, 0, 3).reshape(shard_rows, 3 * width)
+    return (
+        output[None],
+        grad_tokens[None],
+        result_qkv,
+        owned(late[0]),
+        owned(late[1]),
+        result_out,
+        owned(early[0]),
+        owned(early[1]),
+        owned(early[2]),
+        result_up,
+        owned(early[6:10].reshape(-1)),
+        result_down,
+        owned(early[5]),
+        owned(early[3]),
+        owned(early[4]),
+    )
+
+
 def solution(mesh):
-    placed = (
-        P("shard", "seq", None),
-        P("shard"),
-        P("shard", None),
-        P("shard"),
-        P("shard"),
-        P("shard", None),
-        P("shard"),
-        P("shard"),
-        P("shard"),
-        P("shard", None),
-        P("shard"),
-        P("shard", None),
-        P("shard"),
-        P("shard"),
-        P("shard"),
-        P("shard", "seq", None),
-    )
+    seq_count, shard_count = mesh.shape["seq"], mesh.shape["shard"]
+    fast = seq_count == 4 and shard_count == 8
+    if fast:
+        grid = mesh.devices.reshape(seq_count, shard_count // 2, 2)
+        mesh = jax.sharding.Mesh(grid, AXES)
+    shard = ("z", "core") if fast else "shard"
+    vector, matrix, rows = P(shard), P(shard, None), P(shard, "seq", None)
     return jax.shard_map(
-        body,
+        fast_body if fast else body,
         mesh=mesh,
-        in_specs=placed,
+        in_specs=(
+            rows,
+            vector,
+            matrix,
+            vector,
+            vector,
+            matrix,
+            vector,
+            vector,
+            vector,
+            matrix,
+            vector,
+            matrix,
+            vector,
+            vector,
+            vector,
+            rows,
+        ),
         out_specs=(
-            P("shard", "seq", None),
-            P("shard", "seq", None),
-            P("shard", None),
-            P("shard"),
-            P("shard"),
-            P("shard", None),
-            P("shard"),
-            P("shard"),
-            P("shard"),
-            P("shard", None),
-            P("shard"),
-            P("shard", None),
-            P("shard"),
-            P("shard"),
-            P("shard"),
+            rows,
+            rows,
+            matrix,
+            vector,
+            vector,
+            matrix,
+            vector,
+            vector,
+            vector,
+            matrix,
+            vector,
+            matrix,
+            vector,
+            vector,
+            vector,
         ),
         check_vma=False,
     )

time: 711 us -> 381 us (0.54)
  waiting for transfers between devices: 359 us -> 136 us
  matrix products: 83 us -> 0 us
  blocking collectives: 143 us -> 67.8 us
  Pallas kernels: 0 us -> 54.4 us
  starting transfers between devices: 11.5 us -> 57.8 us
  local copies, waits for them, and re-layouts: 64.3 us -> 28.4 us
    reduce_scatter x5 -> x0, waiting for transfers between devices: 207 us -> none  [the longest x1 97.8 us: body(): lax.psum_scatter(grad_w_up, 'shard', scatter_dimension=0, tiled=True)]
    dot_general x26 -> x0, matrix products: 83 us -> none  [the longest x4 16.3 us: contract_rows(): lax.dot_general(left, right, (((0,), (0,)), ((), ())), preferred_element_...]
    unnamed x15 -> x1, waiting for transfers between devices: 76.9 us -> 0.02 us
    ppermute x0 -> x28, waiting for transfers between devices: none -> 71.8 us  [the longest x16 63.1 us: across(): return lax.ppermute(value, 'seq', [(i, i ^ step) for i in range(4)])]
    unnamed x2 -> x0, blocking collectives: 58 us -> none
    all_gather x4 -> x1, waiting for transfers between devices: 55.3 us -> 0.02 us  [fast_body(): gathered = lax.all_gather(quarter, ('z', 'core', 'seq'), axis=0, tiled=True)]
    all_gather x5 -> x0, blocking collectives: 54.9 us -> none  [the longest x1 13 us: body(): lax.all_gather(up_bias, 'shard', axis=0, tiled=True)]
    pallas_call x0 -> x6, Pallas kernels: none -> 54.4 us  [the longest x1 14.8 us: fast_body(): pl.pallas_call(middle_kernel, name='middle', out_shape=(struct((rows, wid...]
  transfers between devices with their start and end apart: 15 -> 37, of which waited for: 10 -> 18; matrix products, arithmetic and copies ran while one was open for 21% -> 10% of each run, Pallas kernels for 0% -> 11%
where the time goes in v1:
time: 381 us; the launch traced here: 377 us
  waiting for transfers between devices  136 us (36%)
  blocking collectives  67.8 us (18%)
  starting transfers between devices  57.8 us (15%)
  Pallas kernels  54.4 us (14%)
  local copies, waits for them, and re-layouts  28.4 us (7%)
  other arithmetic  17.2 us (5%)
  between operations  15.6 us (4%)
    all_to_all x3, blocking collectives, exchange(): return lax.all_to_all(value, axis, split_axis=0, concat_axis=0, tiled=True)  67.8 us
    ppermute x16, waiting for transfers between devices, across(): return lax.ppermute(value, 'seq', [(i, i ^ step) for i in range(4)])  63.1 us
    all_to_all x5, waiting for transfers between devices, spread(): return lax.all_to_all(copies, axis, split_axis=0, concat_axis=0, tiled=True)  56.3 us
    all_to_all x5, starting transfers between devices, spread(): return lax.all_to_all(copies, axis, split_axis=0, concat_axis=0, tiled=True)  20.6 us
    ppermute x16, starting transfers between devices, across(): return lax.ppermute(value, 'seq', [(i, i ^ step) for i in range(4)])  19.2 us
    pallas_call x1, Pallas kernels, fast_body(): pl.pallas_call(middle_kernel, name='middle', out_shape=(struct((rows, wid...  14.8 us
    pallas_call x1, Pallas kernels, fast_body(): pl.pallas_call(attend_forward_kernel, name='attend_forward', out_shape=(s...  12.9 us
    pallas_call x1, Pallas kernels, fast_body(): pl.pallas_call(attend_backward_kernel, name='attend_backward', out_shape=...  11.4 us
  transfers between devices with their start and end apart: 37, of which 18 were waited for; matrix products, arithmetic and copies ran while one was open for 10% of the time, Pallas kernels for 11%

profile of v1, /device:TPU:0, one launch (start us, length us, event | category | flops | bytes accessed | tf_op | source)
XLA Modules:
  0.0 377.0 jit_solution(6531557061249532977)
XLA Ops:
  7.3 1.1 constant_dynamic-slice_fusion.8
  9.4 0.9 broadcast_in_dim.55
  10.3 6.3 %all-to-all-start.1 = ((bf16[4,112,768]{2,1,0:T(8,128)(2,1)}), bf16[4,112,768]{2,1,0:T(8,128)(2,1)S(1)}, u32[]{:S(2)}, u32[]{:S(2)}) async-start(bf16[4,112,768]{2,1,0:T(8,128)(2,1)} %broadcast_in_dim.55), calls=%async_computation.1 | async-start | bytes 1376256 | tf_op jit(solution)/shard_map/all_to_all | solution.py:674
  18.7 22.2 %all-to-all-done.1.own_out = bf16[4,112,768]{2,1,0:T(8,128)(2,1)S(1)} async-done(((bf16[4,112,768]{2,1,0:T(8,128)(2,1)}), bf16[4,112,768]{2,1,0:T(8,128)(2,1)S(1)}, u32[]{:S(2)}, u32[]{:S(2)}) %all-to-all-start.1) | async-done | bytes 688160 | tf_op jit(solution)/shard_map/all_to_all | solution.py:674
  40.8 0.9 broadcast_in_dim.54
  41.7 3.6 all-to-all-start
  45.5 25.8 %all-to-all-done.own = bf16[4,112,576]{2,1,0:T(8,128)(2,1)S(1)} async-done(((bf16[4,112,576]{2,1,0:T(8,128)(2,1)}), bf16[4,112,576]{2,1,0:T(8,128)(2,1)S(1)}, u32[]{:S(2)}, u32[]{:S(2)}) %all-to-all-start) | async-done | bytes 516128 | tf_op jit(solution)/shard_map/all_to_all | solution.py:674
  71.2 1.6 collective-permute-start
  72.8 1.7 collective-permute-start.1
  76.1 11.7 %collective-permute-done.t1 = bf16[256,768]{1,0:T(8,128)(2,1)S(1)} collective-permute-done((bf16[256,768]{1,0:T(8,128)(2,1)S(1)}, bf16[256,768]{1,0:T(8,128)(2,1)S(1)}, u32[]{:S(2)}, u32[]{:S(2)}) %collective-permute-start) | collective-permute-done | bytes 393248 | tf_op jit(solution)/shard_map/ppermute | solution.py:667
  87.8 6.9 %collective-permute-done.1.t2 = bf16[256,768]{1,0:T(8,128)(2,1)S(1)} collective-permute-done((bf16[256,768]{1,0:T(8,128)(2,1)S(1)}, bf16[256,768]{1,0:T(8,128)(2,1)S(1)}, u32[]{:S(2)}, u32[]{:S(2)}) %collective-permute-start.1) | collective-permute-done | bytes 393248 | tf_op jit(solution)/shard_map/ppermute | solution.py:667
  94.8 10.5 %collective-permute-done.2.t3 = bf16[256,768]{1,0:T(8,128)(2,1)S(1)} collective-permute-done((bf16[256,768]{1,0:T(8,128)(2,1)S(1)}, bf16[256,768]{1,0:T(8,128)(2,1)S(1)}, u32[]{:S(2)}, u32[]{:S(2)}) %collective-permute-start.2) | collective-permute-done | bytes 393248 | tf_op jit(solution)/shard_map/ppermute | solution.py:667
  106.1 12.9 %attend_forward.1 = (bf16[1024,576]{1,0:T(8,128)(2,1)}, f32[192,1024]{1,0:T(8,128)}, bf16[256,192]{1,0:T(8,128)(2,1)}, bf16[256,192]{1,0:T(8,128)(2,1)}, bf16[25...) custom-call(s32[3]{0:T(128)} %pad_add_fusion.sc, ...), custom_call_target="tpu_custom_call" | custom-call | tf_op jit(solution)/shard_map/attend_forward/pallas_call | solution.py:703
  118.9 2.6 collective-permute-start.4
  121.9 1.2 collective-permute-start.6
  125.5 3.2 collective-permute-done.5.x2
  129.4 14.8 %middle.1 = (bf16[256,768]{1,0:T(8,128)(2,1)}, f32[256,768]{1,0:T(8,128)}, bf16[256,192]{1,0:T(8,128)(2,1)}, bf16[256,192]{1,0:T(8,128)(2,1)}, bf16[256,192]{1,0...) custom-call(s32[3]{0:T(128)} %pad_add_fusion.sc, ...), custom_call_target="tpu_custom_call" | custom-call | tf_op jit(solution)/shard_map/middle/pallas_call | solution.py:741
  144.2 0.9 collective-permute-start.10
  145.2 1.6 collective-permute-start.8
  146.8 1.0 collective-permute-start.9
  147.8 3.9 %collective-permute-done.10.g3 = bf16[256,192]{1,0:T(8,128)(2,1)S(1)} collective-permute-done((bf16[256,192]{1,0:T(8,128)(2,1)}, bf16[256,192]{1,0:T(8,128)(2,1)S(1)}, u32[]{:S(2)}, u32[]{:S(2)}) %collective-permute-start.10) | collective-permute-done | bytes 98336 | tf_op jit(solution)/shard_map/ppermute | solution.py:667
  151.7 1.9 collective-permute-done.8.g1
  154.7 11.4 %attend_backward.1.dqkv = bf16[1024,576]{1,0:T(8,128)(2,1)} custom-call(s32[3]{0:T(128)} %pad_add_fusion.sc, bf16[1024,576]{1,0:T(8,128)(2,1)} %get-tuple-element.49.qkv, f32[192,1024]{1,0:T(8,128)} %get-tuple-element.50.ctx_t, f32[3,1024]{1,0:T(4,128)} %get-tuple-element.51.lse, bf16[256,192]{1,0:T(8,128)(2,1)} %get-tuple-element.52.g0, ...), custom_call_target="tpu_custom_call" | custom-call | tf_op jit(solution)/shard_map/attend_backward/pallas_call | solution.py:810
  166.2 4.2 %grad_qkv_weight.1 = (bf16[4,96,576]{2,1,0:T(8,128)(2,1)}, bf16[4,96,576]{2,1,0:T(8,128)(2,1)}, f32[1,576]{1,0:T(1,128)}) custom-call(s32[3]{0:T(128)} %pad_add_fusion.sc, bf16[256,768]{1,0:T(8,128)(2,1)} %bitcast.67, bf16[256,768]{1,0:T(8,128)(2,1)} %copy-done.6, bf16[256,768]{1,0:T(8,128)(2,1)} %copy-done.7, bf16[256,768]{1,0:T(8,128)(2,1)} %copy-done.8, ...), custom_call_target="tpu_custom_call" | custom-call | tf_op jit(solution)/shard_map/grad_qkv_weight/pallas_call | solution.py:821
  170.4 2.0 collective-permute-done.14
  172.4 1.1 add_convert_fusion
  173.6 16.8 %all_to_all.57 = bf16[4,96,576]{2,1,0:T(8,128)(2,1)S(1)} all-to-all(bf16[4,96,576]{2,1,0:T(8,128)(2,1)S(1)} %add_convert_fusion), channel_id=1, replica_groups=mesh['seq'=4,'z'=4,'core'=2] {'z'}, dimensions={0} | all-to-all | bytes 884736 | tf_op jit(solution)/shard_map/all_to_all | solution.py:799
  191.1 1.7 broadcast_in_dim.58
  192.8 3.5 all-to-all-start.3
  196.3 1.6 copy-done.1
  197.9 7.4 %weight_grads.1 = (bf16[4,4,96,768]{3,2,1,0:T(8,128)(2,1)}, bf16[4,4,192,384]{3,2,1,0:T(8,128)(2,1)}, bf16[4,192,384]{2,1,0:T(8,128)(2,1)}) custom-call(bf16[256,5760]{1,0:T(8,128)(2,1)} %get-tuple-element.64.keep, bf16[256,5760]{1,0:T(8,128)(2,1)} %copy-done.1), custom_call_target="tpu_custom_call" | custom-call | tf_op jit(solution)/shard_map/weight_grads/pallas_call | solution.py:786
  205.2 19.1 %all_to_all.55 = bf16[4,192,384]{2,1,0:T(8,128)(2,1)S(1)} all-to-all(bf16[4,192,384]{2,1,0:T(8,128)(2,1)} %get-tuple-element.66), channel_id=1, replica_groups=mesh['seq'=4,'z'=4,'core'=2] {'z'}, dimensions={0} | all-to-all | bytes 1179648 | tf_op jit(solution)/shard_map/all_to_all | solution.py:799
  224.3 31.9 %all_to_all.56 = bf16[4,4,192,384]{3,2,1,0:T(8,128)(2,1)} all-to-all(bf16[4,4,192,384]{3,2,1,0:T(8,128)(2,1)} %get-tuple-element.70), channel_id=1, replica_groups=mesh['seq'=4,'z'=4,'core'=2] {'seq'}, dimensions={0} | all-to-all | bytes 4718592 | tf_op jit(solution)/shard_map/all_to_all | solution.py:799
  256.3 3.8 %all-to-all-start.6 = ((bf16[4,4,96,768]{3,2,1,0:T(8,128)(2,1)}), bf16[4,4,96,768]{3,2,1,0:T(8,128)(2,1)S(1)}, u32[]{:S(2)}, u32[]{:S(2)}) async-start(bf16[4,4,96,768]{3,2,1,0:T(8,128)(2,1)} %get-tuple-element.69), calls=%async_computation.6 | async-start | bytes 4718592 | tf_op jit(solution)/shard_map/all_to_all | solution.py:799
  261.4 1.2 collective-permute-done.22
  262.6 2.0 collective-permute-start.23
  265.6 21.1 %collective-permute-done.23 = f32[10,768]{1,0:T(8,128)S(1)} collective-permute-done((f32[10,768]{1,0:T(8,128)S(1)}, f32[10,768]{1,0:T(8,128)S(1)}, u32[]{:S(2)}, u32[]{:S(2)}) %collective-permute-start.23) | collective-permute-done | bytes 30752 | tf_op jit(solution)/shard_map/ppermute | solution.py:667
  287.3 1.5 collective-permute-start.24
  288.8 3.0 reduce_sum.89
  291.8 3.5 all-to-all-start.9
  295.9 1.4 add.111
  297.3 2.0 collective-permute-start.25
  299.7 3.3 collective-permute-done.17
  303.0 1.7 collective-permute-start.18
  304.7 2.6 collective-permute-done.18
  307.3 2.0 collective-permute-start.19
  309.2 3.8 grad_tokens.1
  313.0 1.3 collective-permute-start.11
  314.9 1.6 collective-permute-start.13
  317.3 1.0 collective-permute-start.26
  319.5 2.8 collective-permute-done.26
  322.9 1.3 reduce_sum.87
  324.3 3.8 %all-to-all-start.7 = ((bf16[4,96,768]{2,1,0:T(8,128)(2,1)}), bf16[4,96,768]{2,1,0:T(8,128)(2,1)S(1)}, u32[]{:S(2)}, u32[]{:S(2)}) async-start(bf16[4,96,768]{2,1,0:T(8,128)(2,1)} %reduce_sum.87), calls=%async_computation.7 | async-start | bytes 1179648 | tf_op jit(solution)/shard_map/all_to_all | solution.py:799
  331.3 7.7 %all-to-all-done.7 = bf16[4,96,768]{2,1,0:T(8,128)(2,1)S(1)} async-done(((bf16[4,96,768]{2,1,0:T(8,128)(2,1)}), bf16[4,96,768]{2,1,0:T(8,128)(2,1)S(1)}, u32[]{:S(2)}, u32[]{:S(2)}) %all-to-all-start.7) | async-done | bytes 589856 | tf_op jit(solution)/shard_map/all_to_all | solution.py:799
  339.9 3.5 all-to-all-start.5
  344.8 6.2 %all-to-all-done.5 = bf16[4,2,96,384]{3,2,1,0:T(8,128)(2,1)S(1)} async-done(((bf16[4,2,96,384]{3,2,1,0:T(8,128)(2,1)}), bf16[4,2,96,384]{3,2,1,0:T(8,128)(2,1)S(1)}, u32[]{:S(2)}, u32[]{:S(2)}) %all-to-all-start.5) | async-done | bytes 589856 | tf_op jit(solution)/shard_map/all_to_all | solution.py:674
  350.9 1.1 broadcast_in_dim.61
  352.0 3.7 all-to-all-start.10
  355.8 2.5 fusion
  360.3 1.7 reshape.131
  362.0 0.9 bitcast_select_fusion.3
  363.6 2.2 all-to-all-done.10
  365.8 1.2 fusion.12
  368.4 1.5 reshape.126
  (186 shorter events, 26.8 us)
Async XLA Ops:
  7.2 1.9 copy-start.25
  7.2 1.9 copy-start.26
  7.2 1.9 copy-start.27
  7.2 1.9 copy-start.24
  7.2 1.9 copy-start.28
  7.2 1.9 copy-start.29
  7.2 1.9 copy-start.30
  7.3 2.1 copy-start.13
  7.3 121.4 %all-gather.2.cloned.1.call-start = ((), (), s32[]{:S(2)}) async-start(), calls=%async_computation.11 | async-start | bytes 9732096 | tf_op jit(solution)/shard_map/all_gather | solution.py:684
  9.4 7.3 %copy-start.31 = (bf16[96]{0:T(256)(128)(2,1)S(1)}, bf16[96]{0:T(256)(128)(2,1)}, u32[]{:S(2)}) copy-start(bf16[96]{0:T(256)(128)(2,1)} %param.19) | copy-start | bytes 580
  9.4 7.4 %copy-start.32 = (bf16[96]{0:T(256)(128)(2,1)S(1)}, bf16[96]{0:T(256)(128)(2,1)}, u32[]{:S(2)}) copy-start(bf16[96]{0:T(256)(128)(2,1)} %param.20) | copy-start | bytes 580
  9.4 7.8 %copy-start.12 = (bf16[96,2304]{1,0:T(8,128)(2,1)S(1)}, bf16[96,2304]{1,0:T(8,128)(2,1)}, u32[]{:S(2)}) copy-start(bf16[96,2304]{1,0:T(8,128)(2,1)} %param.18) | copy-start | bytes 1327108
  10.3 30.5 %all-to-all-start.1 = ((bf16[4,112,768]{2,1,0:T(8,128)(2,1)}), bf16[4,112,768]{2,1,0:T(8,128)(2,1)S(1)}, u32[]{:S(2)}, u32[]{:S(2)}) async-start(bf16[4,112,768]{2,1,0:T(8,128)(2,1)} %broadcast_in_dim.55), calls=%async_computation.1 | async-start | bytes 1376256 | tf_op jit(solution)/shard_map/all_to_all | solution.py:674
  18.5 52.7 %copy-start = (bf16[1,256,768]{2,1,0:T(8,128)(2,1)S(1)}, bf16[1,256,768]{2,1,0:T(8,128)(2,1)}, u32[]{:S(2)}) copy-start(bf16[1,256,768]{2,1,0:T(8,128)(2,1)} %param.16) | copy-start | bytes 1179652
  40.8 78.1 %copy-start.2 = (bf16[4,112,768]{2,1,0:T(8,128)(2,1)}, bf16[4,112,768]{2,1,0:T(8,128)(2,1)S(1)}, u32[]{:S(2)}) copy-start(bf16[4,112,768]{2,1,0:T(8,128)(2,1)S(1)} %all-to-all-done.1.own_out) | copy-start | bytes 2064388
  41.7 29.5 %all-to-all-start = ((bf16[4,112,576]{2,1,0:T(8,128)(2,1)}), bf16[4,112,576]{2,1,0:T(8,128)(2,1)S(1)}, u32[]{:S(2)}, u32[]{:S(2)}) async-start(bf16[4,112,576]{2,1,0:T(8,128)(2,1)} %broadcast_in_dim.54), calls=%async_computation | async-start | bytes 1146880 | tf_op jit(solution)/shard_map/all_to_all | solution.py:674
  45.4 77.7 %collective-permute-start.7 = (bf16[4,112,768]{2,1,0:T(8,128)(2,1)S(1)}, bf16[4,112,768]{2,1,0:T(8,128)(2,1)}, u32[]{:S(2)}, u32[]{:S(2)}) collective-permute-start(bf16[4,112,768]{2,1,0:T(8,128)(2,1)S(1)} %all-to-all-done.1.own_out), channel_id=1, source_target_pairs={{0,1},{1,0},{2,3},{3,2},{4,5},{5,4},{6,7},{7,6},{8,9},{9,8},{10,11... | collective-permute-start | bytes 2064392 | tf_op jit(solution)/shard_map/ppermute | solution.py:670
  71.2 34.1 %copy-start.3 = (bf16[4,112,576]{2,1,0:T(8,128)(2,1)}, bf16[4,112,576]{2,1,0:T(8,128)(2,1)S(1)}, u32[]{:S(2)}) copy-start(bf16[4,112,576]{2,1,0:T(8,128)(2,1)S(1)} %all-to-all-done.own) | copy-start | bytes 1548292
  71.2 34.1 %collective-permute-start.3 = (bf16[4,112,576]{2,1,0:T(8,128)(2,1)S(1)}, bf16[4,112,576]{2,1,0:T(8,128)(2,1)}, u32[]{:S(2)}, u32[]{:S(2)}) collective-permute-start(bf16[4,112,576]{2,1,0:T(8,128)(2,1)S(1)} %all-to-all-done.own), channel_id=1, source_target_pairs={{0,1},{1,0},{2,3},{3,2},{4,5},{5,4},{6,7},{7,6},{8,9},{9,8},{10,11... | collective-permute-start | bytes 1548296 | tf_op jit(solution)/shard_map/ppermute | solution.py:670
  71.2 16.6 %collective-permute-start = (bf16[256,768]{1,0:T(8,128)(2,1)S(1)}, bf16[256,768]{1,0:T(8,128)(2,1)S(1)}, u32[]{:S(2)}, u32[]{:S(2)}) collective-permute-start(bf16[256,768]{1,0:T(8,128)(2,1)S(1)} %bitcast.68), channel_id=1, source_target_pairs={{0,8},{8,0},{16,24},{24,16},{1,9},{9,1},{17,25},{25,17},{2,10},{10... | collective-permute-start | bytes 1179656 | tf_op jit(solution)/shard_map/ppermute | solution.py:667
  72.8 22.0 %collective-permute-start.1 = (bf16[256,768]{1,0:T(8,128)(2,1)S(1)}, bf16[256,768]{1,0:T(8,128)(2,1)S(1)}, u32[]{:S(2)}, u32[]{:S(2)}) collective-permute-start(bf16[256,768]{1,0:T(8,128)(2,1)S(1)} %bitcast.69), channel_id=1, source_target_pairs={{0,16},{8,24},{16,0},{24,8},{1,17},{9,25},{17,1},{25,9},{2,18},{10... | collective-permute-start | bytes 1179656 | tf_op jit(solution)/shard_map/ppermute | solution.py:667
  74.5 30.8 %collective-permute-start.2 = (bf16[256,768]{1,0:T(8,128)(2,1)S(1)}, bf16[256,768]{1,0:T(8,128)(2,1)S(1)}, u32[]{:S(2)}, u32[]{:S(2)}) collective-permute-start(bf16[256,768]{1,0:T(8,128)(2,1)S(1)} %bitcast.70), channel_id=1, source_target_pairs={{0,24},{8,16},{16,8},{24,0},{1,25},{9,17},{17,9},{25,1},{2,26},{10... | collective-permute-start | bytes 1179656 | tf_op jit(solution)/shard_map/ppermute | solution.py:667
  87.8 17.5 %copy-start.6 = (bf16[256,768]{1,0:T(8,128)(2,1)}, bf16[256,768]{1,0:T(8,128)(2,1)S(1)}, u32[]{:S(2)}) copy-start(bf16[256,768]{1,0:T(8,128)(2,1)S(1)} %collective-permute-done.t1) | copy-start | bytes 1179652
  94.8 10.6 %copy-start.7 = (bf16[256,768]{1,0:T(8,128)(2,1)}, bf16[256,768]{1,0:T(8,128)(2,1)S(1)}, u32[]{:S(2)}) copy-start(bf16[256,768]{1,0:T(8,128)(2,1)S(1)} %collective-permute-done.1.t2) | copy-start | bytes 1179652
  118.9 6.5 %collective-permute-start.4 = (bf16[256,192]{1,0:T(8,128)(2,1)}, bf16[256,192]{1,0:T(8,128)(2,1)S(1)}, u32[]{:S(2)}, u32[]{:S(2)}) collective-permute-start(bf16[256,192]{1,0:T(8,128)(2,1)} %get-tuple-element.44), channel_id=1, source_target_pairs={{0,8},{8,0},{16,24},{24,16},{1,9},{9,1},{17,25},{25,17},{2,10},{10... | collective-permute-start | bytes 294920 | tf_op jit(solution)/shard_map/ppermute | solution.py:667
  121.5 7.1 %collective-permute-start.5 = (bf16[256,192]{1,0:T(8,128)(2,1)}, bf16[256,192]{1,0:T(8,128)(2,1)S(1)}, u32[]{:S(2)}, u32[]{:S(2)}) collective-permute-start(bf16[256,192]{1,0:T(8,128)(2,1)} %get-tuple-element.45), channel_id=1, source_target_pairs={{0,16},{8,24},{16,0},{24,8},{1,17},{9,25},{17,1},{25,9},{2,18},{10... | collective-permute-start | bytes 294920 | tf_op jit(solution)/shard_map/ppermute | solution.py:667
  121.9 6.8 %collective-permute-start.6 = (bf16[256,192]{1,0:T(8,128)(2,1)}, bf16[256,192]{1,0:T(8,128)(2,1)S(1)}, u32[]{:S(2)}, u32[]{:S(2)}) collective-permute-start(bf16[256,192]{1,0:T(8,128)(2,1)} %get-tuple-element.46), channel_id=1, source_target_pairs={{0,24},{8,16},{16,8},{24,0},{1,25},{9,17},{17,9},{25,1},{2,26},{10... | collective-permute-start | bytes 294920 | tf_op jit(solution)/shard_map/ppermute | solution.py:667
  125.5 3.2 copy-start.14
  144.2 52.1 %collective-permute-start.20 = (bf16[256,5760]{1,0:T(8,128)(2,1)}, bf16[256,5760]{1,0:T(8,128)(2,1)S(1)}, u32[]{:S(2)}, u32[]{:S(2)}) collective-permute-start(bf16[256,5760]{1,0:T(8,128)(2,1)} %get-tuple-element.65), channel_id=1, source_target_pairs={{0,1},{1,0},{2,3},{3,2},{4,5},{5,4},{6,7},{7,6},{8,9},{9,8},{10,11... | collective-permute-start | bytes 8847368 | tf_op jit(solution)/shard_map/ppermute | solution.py:670
  144.2 7.5 %collective-permute-start.10 = (bf16[256,192]{1,0:T(8,128)(2,1)}, bf16[256,192]{1,0:T(8,128)(2,1)S(1)}, u32[]{:S(2)}, u32[]{:S(2)}) collective-permute-start(bf16[256,192]{1,0:T(8,128)(2,1)} %get-tuple-element.55), channel_id=1, source_target_pairs={{0,24},{8,16},{16,8},{24,0},{1,25},{9,17},{17,9},{25,1},{2,26},{10... | collective-permute-start | bytes 294920 | tf_op jit(solution)/shard_map/ppermute | solution.py:667
  145.2 8.4 %collective-permute-start.8 = (bf16[256,192]{1,0:T(8,128)(2,1)}, bf16[256,192]{1,0:T(8,128)(2,1)S(1)}, u32[]{:S(2)}, u32[]{:S(2)}) collective-permute-start(bf16[256,192]{1,0:T(8,128)(2,1)} %get-tuple-element.53), channel_id=1, source_target_pairs={{0,8},{8,0},{16,24},{24,16},{1,9},{9,1},{17,25},{25,17},{2,10},{10... | collective-permute-start | bytes 294920 | tf_op jit(solution)/shard_map/ppermute | solution.py:667
  146.8 7.3 %collective-permute-start.9 = (bf16[256,192]{1,0:T(8,128)(2,1)}, bf16[256,192]{1,0:T(8,128)(2,1)S(1)}, u32[]{:S(2)}, u32[]{:S(2)}) collective-permute-start(bf16[256,192]{1,0:T(8,128)(2,1)} %get-tuple-element.54), channel_id=1, source_target_pairs={{0,16},{8,24},{16,0},{24,8},{1,17},{9,25},{17,1},{25,9},{2,18},{10... | collective-permute-start | bytes 294920 | tf_op jit(solution)/shard_map/ppermute | solution.py:667
  151.7 2.4 copy-start.17
  170.4 2.1 collective-permute-start.14
  192.8 12.4 %all-to-all-start.3 = ((bf16[4,96,576]{2,1,0:T(8,128)(2,1)}), bf16[4,96,576]{2,1,0:T(8,128)(2,1)S(1)}, u32[]{:S(2)}, u32[]{:S(2)}) async-start(bf16[4,96,576]{2,1,0:T(8,128)(2,1)} %broadcast_in_dim.58), calls=%async_computation.3 | async-start | bytes 983040 | tf_op jit(solution)/shard_map/all_to_all | solution.py:674
  196.3 1.6 copy-start.1
  205.2 51.0 %copy-start.4 = (bf16[4,96,576]{2,1,0:T(8,128)(2,1)}, bf16[4,96,576]{2,1,0:T(8,128)(2,1)S(1)}, u32[]{:S(2)}) copy-start(bf16[4,96,576]{2,1,0:T(8,128)(2,1)S(1)} %all-to-all-done.3) | copy-start | bytes 1327108
  256.2 4.3 %copy-start.22 = (f32[1,3072]{1,0:T(1,128)S(1)}, f32[1,3072]{1,0:T(1,128)}, u32[]{:S(2)}) copy-start(f32[1,3072]{1,0:T(1,128)} %get-tuple-element.68) | copy-start | bytes 36868
  256.3 5.0 %copy-start.21 = (f32[8,768]{1,0:T(8,128)S(1)}, f32[8,768]{1,0:T(8,128)}, u32[]{:S(2)}) copy-start(f32[8,768]{1,0:T(8,128)} %get-tuple-element.67) | copy-start | bytes 73732
  256.3 8.4 %copy-start.23 = (f32[1,576]{1,0:T(1,128)S(1)}, f32[1,576]{1,0:T(1,128)}, u32[]{:S(2)}) copy-start(f32[1,576]{1,0:T(1,128)} %get-tuple-element.63) | copy-start | bytes 6916
  256.3 35.5 %all-to-all-start.6 = ((bf16[4,4,96,768]{3,2,1,0:T(8,128)(2,1)}), bf16[4,4,96,768]{3,2,1,0:T(8,128)(2,1)S(1)}, u32[]{:S(2)}, u32[]{:S(2)}) async-start(bf16[4,4,96,768]{3,2,1,0:T(8,128)(2,1)} %get-tuple-element.69), calls=%async_computation.6 | async-start | bytes 4718592 | tf_op jit(solution)/shard_map/all_to_all | solution.py:799
  261.3 1.3 collective-permute-start.22
  262.6 24.1 %collective-permute-start.23 = (f32[10,768]{1,0:T(8,128)S(1)}, f32[10,768]{1,0:T(8,128)S(1)}, u32[]{:S(2)}, u32[]{:S(2)}) collective-permute-start(f32[10,768]{1,0:T(8,128)S(1)} %fusion.10), channel_id=1, source_target_pairs={{0,8},{8,0},{16,24},{24,16},{1,9},{9,1},{17,25},{25,17},{2,10},{10... | collective-permute-start | bytes 92168 | tf_op jit(solution)/shard_map/ppermute | solution.py:667
  265.6 29.7 %collective-permute-start.15 = (f32[2,768]{1,0:T(2,128)}, f32[2,768]{1,0:T(2,128)S(1)}, u32[]{:S(2)}, u32[]{:S(2)}) collective-permute-start(f32[2,768]{1,0:T(2,128)} %pad_maximum_fusion.3), channel_id=1, source_target_pairs={{0,1},{1,0},{2,3},{3,2},{4,5},{5,4},{6,7},{7,6},{8,9},{9,8},{10,11... | collective-permute-start | bytes 18440 | tf_op jit(solution)/shard_map/ppermute | solution.py:670
  287.3 8.6 %collective-permute-start.24 = (f32[10,768]{1,0:T(8,128)}, f32[10,768]{1,0:T(8,128)}, u32[]{:S(2)}, u32[]{:S(2)}) collective-permute-start(f32[10,768]{1,0:T(8,128)} %add.110), channel_id=1, source_target_pairs={{0,16},{8,24},{16,0},{24,8},{1,17},{9,25},{17,1},{25,9},{2,18},{10... | collective-permute-start | bytes 92168 | tf_op jit(solution)/shard_map/ppermute | solution.py:667
  291.8 32.5 %all-to-all-start.9 = ((bf16[4,192,384]{2,1,0:T(8,128)(2,1)}), bf16[4,192,384]{2,1,0:T(8,128)(2,1)S(1)}, u32[]{:S(2)}, u32[]{:S(2)}) async-start(bf16[4,192,384]{2,1,0:T(8,128)(2,1)} %reduce_sum.89), calls=%async_computation.9 | async-start | bytes 1179648 | tf_op jit(solution)/shard_map/all_to_all | solution.py:799
  295.3 4.0 %collective-permute-start.16 = (f32[2,768]{1,0:T(2,128)S(1)}, f32[2,768]{1,0:T(2,128)S(1)}, u32[]{:S(2)}, u32[]{:S(2)}) collective-permute-start(f32[2,768]{1,0:T(2,128)S(1)} %fusion.11), channel_id=1, source_target_pairs={{0,8},{8,0},{16,24},{24,16},{1,9},{9,1},{17,25},{25,17},{2,10},{10... | collective-permute-start | bytes 18440 | tf_op jit(solution)/shard_map/ppermute | solution.py:667
  297.3 19.1 %collective-permute-start.25 = (f32[10,768]{1,0:T(8,128)}, f32[10,768]{1,0:T(8,128)}, u32[]{:S(2)}, u32[]{:S(2)}) collective-permute-start(f32[10,768]{1,0:T(8,128)} %add.111), channel_id=1, source_target_pairs={{0,2},{2,0},{4,6},{6,4},{1,3},{3,1},{5,7},{7,5},{8,10},{10,8},{12,... | collective-permute-start | bytes 92168 | tf_op jit(solution)/shard_map/ppermute | solution.py:864
  299.3 3.7 collective-permute-start.17
  303.0 4.2 %collective-permute-start.18 = (f32[2,768]{1,0:T(2,128)S(1)}, f32[2,768]{1,0:T(2,128)S(1)}, u32[]{:S(2)}, u32[]{:S(2)}) collective-permute-start(f32[2,768]{1,0:T(2,128)S(1)} %add.103), channel_id=1, source_target_pairs={{0,2},{2,0},{4,6},{6,4},{1,3},{3,1},{5,7},{7,5},{8,10},{10,8},{12,... | collective-permute-start | bytes 18440 | tf_op jit(solution)/shard_map/ppermute | solution.py:864
  307.3 11.0 %collective-permute-start.19 = (f32[2,768]{1,0:T(2,128)S(1)}, f32[2,768]{1,0:T(2,128)S(1)}, u32[]{:S(2)}, u32[]{:S(2)}) collective-permute-start(f32[2,768]{1,0:T(2,128)S(1)} %add.104), channel_id=1, source_target_pairs={{0,4},{2,6},{4,0},{6,2},{1,5},{3,7},{5,1},{7,3},{8,12},{10,14},{12... | collective-permute-start | bytes 18440 | tf_op jit(solution)/shard_map/ppermute | solution.py:864
  313.0 42.7 %collective-permute-start.11 = (bf16[256,768]{1,0:T(8,128)(2,1)}, bf16[256,768]{1,0:T(8,128)(2,1)}, u32[]{:S(2)}, u32[]{:S(2)}) collective-permute-start(bf16[256,768]{1,0:T(8,128)(2,1)} %get-tuple-element.58), channel_id=1, source_target_pairs={{0,8},{8,0},{16,24},{24,16},{1,9},{9,1},{17,25},{25,17},{2,10},{10... | collective-permute-start | bytes 1179656 | tf_op jit(solution)/shard_map/ppermute | solution.py:667
  314.3 41.4 %collective-permute-start.12 = (bf16[256,768]{1,0:T(8,128)(2,1)}, bf16[256,768]{1,0:T(8,128)(2,1)}, u32[]{:S(2)}, u32[]{:S(2)}) collective-permute-start(bf16[256,768]{1,0:T(8,128)(2,1)} %get-tuple-element.59), channel_id=1, source_target_pairs={{0,16},{8,24},{16,0},{24,8},{1,17},{9,25},{17,1},{25,9},{2,18},{10... | collective-permute-start | bytes 1179656 | tf_op jit(solution)/shard_map/ppermute | solution.py:667
  314.9 40.9 %collective-permute-start.13 = (bf16[256,768]{1,0:T(8,128)(2,1)}, bf16[256,768]{1,0:T(8,128)(2,1)}, u32[]{:S(2)}, u32[]{:S(2)}) collective-permute-start(bf16[256,768]{1,0:T(8,128)(2,1)} %get-tuple-element.60), channel_id=1, source_target_pairs={{0,24},{8,16},{16,8},{24,0},{1,25},{9,17},{17,9},{25,1},{2,26},{10... | collective-permute-start | bytes 1179656 | tf_op jit(solution)/shard_map/ppermute | solution.py:667
  317.3 5.0 %collective-permute-start.26 = (f32[10,768]{1,0:T(8,128)S(1)}, f32[10,768]{1,0:T(8,128)S(1)}, u32[]{:S(2)}, u32[]{:S(2)}) collective-permute-start(f32[10,768]{1,0:T(8,128)S(1)} %add.112), channel_id=1, source_target_pairs={{0,4},{2,6},{4,0},{6,2},{1,5},{3,7},{5,1},{7,3},{8,12},{10,14},{12... | collective-permute-start | bytes 92168 | tf_op jit(solution)/shard_map/ppermute | solution.py:864
  324.3 3.8 %copy-start.20 = (f32[10,768]{1,0:T(8,128)S(1)}, f32[10,768]{1,0:T(8,128)}, u32[]{:S(2)}) copy-start(f32[10,768]{1,0:T(8,128)} %add.113) | copy-start | bytes 92164
  324.3 14.7 %all-to-all-start.7 = ((bf16[4,96,768]{2,1,0:T(8,128)(2,1)}), bf16[4,96,768]{2,1,0:T(8,128)(2,1)S(1)}, u32[]{:S(2)}, u32[]{:S(2)}) async-start(bf16[4,96,768]{2,1,0:T(8,128)(2,1)} %reduce_sum.87), calls=%async_computation.7 | async-start | bytes 1179648 | tf_op jit(solution)/shard_map/all_to_all | solution.py:799
  331.2 13.5 %collective-permute-start.27 = (bf16[96,384]{1,0:T(8,128)(2,1)S(1)}, bf16[96,384]{1,0:T(8,128)(2,1)S(1)}, u32[]{:S(2)}, u32[]{:S(2)}) collective-permute-start(bf16[96,384]{1,0:T(8,128)(2,1)S(1)} %dynamic-slice_bitcast_fusion), channel_id=1, source_target_pairs={{0,1},{1,0},{2,3},{3,2},{4,5},{5,4},{6,7},{7,6},{8,9},{9,8},{10,11... | collective-permute-start | bytes 221192 | tf_op jit(solution)/shard_map/ppermute | solution.py:670
  339.9 11.1 %all-to-all-start.5 = ((bf16[4,2,96,384]{3,2,1,0:T(8,128)(2,1)}), bf16[4,2,96,384]{3,2,1,0:T(8,128)(2,1)S(1)}, u32[]{:S(2)}, u32[]{:S(2)}) async-start(bf16[4,2,96,384]{3,2,1,0:T(8,128)(2,1)} %broadcast_in_dim.60), calls=%async_computation.5 | async-start | bytes 1179648 | tf_op jit(solution)/shard_map/all_to_all | solution.py:674
  352.0 3.7 copy-start.9
  352.0 13.8 %all-to-all-start.10 = ((bf16[4,192,768]{2,1,0:T(8,128)(2,1)}), bf16[4,192,768]{2,1,0:T(8,128)(2,1)S(1)}, u32[]{:S(2)}, u32[]{:S(2)}) async-start(bf16[4,192,768]{2,1,0:T(8,128)(2,1)} %broadcast_in_dim.61), calls=%async_computation.10 | async-start | bytes 2359296 | tf_op jit(solution)/shard_map/all_to_all | solution.py:674
  355.8 2.5 copy-start.5
  359.3 2.6 collective-permute-start.21
  360.3 1.7 copy-start.11
  (6 other events, 4.1 us)
Sparse Core Ops, SparseCore 0:
  11.6 108.0 all-gather.1
